TPU v7x, 512 devices: a whole 4x4x16 slice. The times are simulated.
512 devices in a mesh: rep: 64 (over z, x_lo, core), dom: 8 (over x_hi, y).
Axes of the slice: x: 4 (x_hi: 2, x_lo: 2; x = x_hi * 2 + x_lo), y: 4, z: 16, core: 2. Of those that a mesh axis runs over, the one named last changes fastest.
Arguments:
- particle_locations: float32 [64, 3, 8192], P('rep', None, 'dom'), may hold values from 0 to 1.5
- particle_speeds: float32 [64, 3, 8192], P('rep', None, 'dom'), may hold values from -6 to 6
- current_pushes: float32 [64, 3, 8192], P('rep', None, 'dom'), may hold values from -6 to 6
- particle_kinds: int32 [64, 8192], P('rep', 'dom'), may hold values from 0 to 15
- halo_particle_labels: int32 [64, 6144], P('rep', 'dom'), may hold values from 0 to 1023
- adjacent_block_labels: int32 [64, 64, 4], P('rep', 'dom'), may hold values from 0 to 13
- adjacent_place_totals: int32 [64, 64], P('rep', 'dom'), may hold values from 1 to 4, as said below
- kind_vectors: bfloat16 [16, 128], replicated, may hold values from -6 to 6
- kind_inertia: float32 [16], replicated, may hold values from 1 to 4
- stepwise_distance_coefficients: float32 [2, 8, 128], replicated, may hold values from -2 to 2
- signal_scaling_factors: float32 [2, 128], replicated, may hold values from 0.1 to 1.9
- feature_blend_coefficients: bfloat16 [2, 128, 128], replicated, may hold values from -0.5 to 0.5
- target_projection_array: bfloat16 [128, 128], replicated, may hold values from -0.5 to 0.5
- source_projection_array: bfloat16 [128, 128], replicated, may hold values from -0.5 to 0.5
- push_distance_taper: float32 [8], replicated, may hold values from -4 to 4
- thermal_levels: float32 [64], replicated, may hold values from 0.5 to 2
- granted_swaps: int32 [64], replicated, may hold values from 0 to 63, as said below
Outputs:
- positions_out: float32 [64, 3, 8192], P('rep', None, 'dom')
- velocities_out: float32 [64, 3, 8192], P('rep', None, 'dom')
- forces_out: float32 [64, 3, 8192], P('rep', None, 'dom')
Inputs may be any that keep to these rules, and one draw needn't show every extreme that they name: `halo_particle_labels`: each domain's block of 768 entries: the first 384 name its atoms imported by the next lower domain, the last 384 those imported by the next higher domain. `adjacent_block_labels`: numbers below 8 are the domain's own tiles; the rest are the imported atoms' tiles in extended order. `adjacent_place_totals`: in every replica some domain has all its tiles at 4 live slots. `granted_swaps`: each replica's partner is itself or a ladder neighbour, and the partner's partner is the replica. The pairs (0, 1), (31, 32) and (62, 63) are always accepted.
All inputs are finite; a program needn't handle non-finite values.
Results may differ from a plain program's by a relative error of at most 0.0067.
Values may be sent and summed in bfloat16 or wider, within the bound.
A program may use at most 64 MiB of HBM per device.

v0:
```python
import math

import jax
import jax.numpy as jnp
from jax import lax
from jax.sharding import PartitionSpec as P

NB = 8
TILE = 128
NEI = 4


slab_width = 1.5
time_step = 0.5
basis_width = 0.3
norm_eps = 1e-06


def with_halo(cells, sides, width):
    for axis, dim in sides:
        count = lax.axis_size(axis)
        head = lax.slice_in_dim(cells, 0, width, axis=dim)
        tail = lax.slice_in_dim(cells, cells.shape[dim] - width, cells.shape[dim], axis=dim)
        cells = jnp.concatenate(
            [
                lax.ppermute(tail, axis, [(i, (i + 1) % count) for i in range(count)]),
                cells,
                lax.ppermute(head, axis, [((i + 1) % count, i) for i in range(count)]),
            ],
            axis=dim,
        )
    return cells


def from_behind(array, axis, by):
    count = lax.axis_size(axis)
    pairs = [(i, i + by) for i in range(count) if 0 <= i + by < count]
    return lax.ppermute(array, axis, pairs)


def slot_basis(near_pos, far_pos, live_flags):
    offsets = far_pos[:, :, None, :] - near_pos[:, None, :, None]
    distance = jnp.sqrt(jnp.sum(offsets * offsets, axis=0))
    centers = basis_width * jnp.arange(NB, dtype=jnp.float32)
    scaled = (distance[:, None, :, :] - centers[None, :, None, None]) / basis_width
    return (jnp.exp(-scaled * scaled) * live_flags[:, None, None, None]).astype(jnp.bfloat16)


def species_onehot(labels, width):
    return labels[:, None] == jnp.arange(width, dtype=jnp.int32)[None, :]


def embed_rows(labels, kind_vectors):
    onehot = species_onehot(labels, kind_vectors.shape[0]).astype(jnp.bfloat16)
    return jnp.dot(onehot, kind_vectors, preferred_element_type=jnp.float32).astype(jnp.bfloat16)


def inverse_mass(labels, kind_inertia):
    chosen_mass = jnp.where(
        species_onehot(labels, kind_inertia.shape[0]), kind_inertia[None, :], 0.0
    )
    return 1.0 / jnp.sum(chosen_mass, axis=1)


def tile_geometry(ext_pos, tile_lists, live_counts):
    tile_total = tile_lists.shape[0]
    near_all = jnp.transpose(
        ext_pos[:, : tile_total * TILE].reshape(3, tile_total, TILE), (1, 0, 2)
    )
    ext_tiled = ext_pos.reshape(3, -1, TILE)
    far_all = jnp.transpose(jnp.take(ext_tiled, tile_lists, axis=1), (1, 0, 2, 3))
    live_all = (jnp.arange(NEI, dtype=jnp.int32)[None, :] < live_counts[:, None]).astype(
        jnp.float32
    )
    return (near_all, far_all, live_all)


def tile_messages(geometry, ext_hidden, tile_lists, radial_row):
    near_all, far_all, live_all = geometry
    channels = ext_hidden.shape[1]
    feat_all = jnp.take(ext_hidden.reshape(-1, TILE, channels), tile_lists, axis=0)

    def one_tile(items):
        near_pos, far_pos, live_flags, far_feat = items
        basis_val = slot_basis(near_pos, far_pos, live_flags)
        summed = jnp.einsum(
            "kbij,kjc->bic", basis_val, far_feat, preferred_element_type=jnp.float32
        )
        return jnp.einsum("bic,bc->ic", summed, radial_row, precision=lax.Precision.HIGHEST)

    result = lax.map(one_tile, (near_all, far_all, live_all, feat_all))
    return result.reshape(-1, channels)


def refresh(hidden, messages, gain_row, mix_matrix):
    inverse = lax.rsqrt(jnp.mean(messages * messages, axis=-1, keepdims=True) + norm_eps)
    activation = jax.nn.silu(messages * inverse * gain_row).astype(jnp.bfloat16)
    return (
        hidden.astype(jnp.float32)
        + jnp.dot(activation, mix_matrix, preferred_element_type=jnp.float32)
    ).astype(jnp.bfloat16)


def tile_forces(geometry, query, ext_keys, tile_lists, push_distance_taper):
    near_all, far_all, live_all = geometry
    channels = query.shape[1]
    factor = 1.0 / math.sqrt(channels * NEI * TILE)
    asking_all = query.reshape(-1, TILE, channels)
    keys_all = jnp.take(ext_keys.reshape(-1, TILE, channels), tile_lists, axis=0)

    def one_tile(items):
        near_pos, far_pos, live_flags, asking, far_keys = items
        basis_val = slot_basis(near_pos, far_pos, live_flags)
        envelope = jnp.einsum(
            "kbij,b->kij",
            basis_val.astype(jnp.float32),
            push_distance_taper,
            precision=lax.Precision.HIGHEST,
        )
        scores = jnp.einsum("ic,kjc->kij", asking, far_keys, preferred_element_type=jnp.float32)
        pair_weight = scores * envelope * factor
        return (
            jnp.einsum("dkj,kij->di", far_pos, pair_weight, precision=lax.Precision.HIGHEST)
            - near_pos * jnp.sum(pair_weight, axis=(0, 2))[None, :]
        )

    result = lax.map(one_tile, (near_all, far_all, live_all, asking_all, keys_all))
    return jnp.transpose(result, (1, 0, 2)).reshape(3, -1)


def evaluate(
    displaced,
    labels,
    ghosts,
    tile_lists,
    live_counts,
    kind_vectors,
    stepwise_distance_coefficients,
    signal_scaling_factors,
    feature_blend_coefficients,
    target_projection_array,
    source_projection_array,
    push_distance_taper,
):
    ghost_count = ghosts.shape[0] // 2
    shift_vec = slab_width * (jnp.arange(3, dtype=jnp.int32) == 0).astype(jnp.float32)[:, None]
    packed_pos = jnp.take(displaced, ghosts, axis=1)
    bordered_pos = with_halo(packed_pos, (("dom", 1),), ghost_count)
    ext_pos = jnp.concatenate(
        [
            displaced,
            bordered_pos[:, :ghost_count] - shift_vec,
            bordered_pos[:, 3 * ghost_count :] + shift_vec,
        ],
        axis=1,
    )
    geometry = tile_geometry(ext_pos, tile_lists, live_counts)
    hidden = embed_rows(labels, kind_vectors)
    bordered_start = with_halo(jnp.take(hidden, ghosts, axis=0), (("dom", 0),), ghost_count)
    ext_hidden = jnp.concatenate(
        [hidden, bordered_start[:ghost_count], bordered_start[3 * ghost_count :]], axis=0
    )
    messages = tile_messages(geometry, ext_hidden, tile_lists, stepwise_distance_coefficients[0])
    hidden = refresh(hidden, messages, signal_scaling_factors[0], feature_blend_coefficients[0])
    bordered_middle = with_halo(jnp.take(hidden, ghosts, axis=0), (("dom", 0),), ghost_count)
    ext_hidden = jnp.concatenate(
        [hidden, bordered_middle[:ghost_count], bordered_middle[3 * ghost_count :]], axis=0
    )
    messages = tile_messages(geometry, ext_hidden, tile_lists, stepwise_distance_coefficients[1])
    hidden = refresh(hidden, messages, signal_scaling_factors[1], feature_blend_coefficients[1])
    query = jnp.dot(hidden, target_projection_array, preferred_element_type=jnp.float32).astype(
        jnp.bfloat16
    )
    bordered_final = with_halo(jnp.take(hidden, ghosts, axis=0), (("dom", 0),), ghost_count)
    final_ext = jnp.concatenate(
        [hidden, bordered_final[:ghost_count], bordered_final[3 * ghost_count :]], axis=0
    )
    ext_keys = jnp.dot(
        final_ext, source_projection_array, preferred_element_type=jnp.float32
    ).astype(jnp.bfloat16)
    return tile_forces(geometry, query, ext_keys, tile_lists, push_distance_taper)


def pick_partner(own_parts, low_parts, high_parts, swap_counterpart, thermal_copy_entry):
    return tuple(
        (
            jnp.where(
                swap_counterpart == thermal_copy_entry + 1,
                high_part,
                jnp.where(swap_counterpart == thermal_copy_entry - 1, low_part, own_part),
            )
            for own_part, low_part, high_part in zip(own_parts, low_parts, high_parts)
        )
    )


def local(
    particle_locations,
    particle_speeds,
    current_pushes,
    particle_kinds,
    halo_particle_labels,
    adjacent_block_labels,
    adjacent_place_totals,
    kind_vectors,
    kind_inertia,
    stepwise_distance_coefficients,
    signal_scaling_factors,
    feature_blend_coefficients,
    target_projection_array,
    source_projection_array,
    push_distance_taper,
    thermal_levels,
    granted_swaps,
):
    coords = particle_locations[0]
    speeds = particle_speeds[0]
    old_force = current_pushes[0]
    labels = particle_kinds[0]
    ghosts = halo_particle_labels[0]
    tile_lists = adjacent_block_labels[0]
    live_counts = adjacent_place_totals[0]
    thermal_copy_entry = lax.axis_index("rep")
    swap_counterpart = granted_swaps[thermal_copy_entry]
    thermal_quotient = jnp.sqrt(
        thermal_levels[thermal_copy_entry] / thermal_levels[swap_counterpart]
    )
    inv_mass = inverse_mass(labels, kind_inertia)
    displaced = (
        coords + time_step * speeds + 0.5 * time_step * time_step * old_force * inv_mass[None, :]
    )
    half_speed = speeds + 0.5 * time_step * old_force * inv_mass[None, :]
    updated_push = evaluate(
        displaced,
        labels,
        ghosts,
        tile_lists,
        live_counts,
        kind_vectors,
        stepwise_distance_coefficients,
        signal_scaling_factors,
        feature_blend_coefficients,
        target_projection_array,
        source_projection_array,
        push_distance_taper,
    )
    updated_velocity = half_speed + 0.5 * time_step * updated_push * inv_mass[None, :]
    lower_state = (
        from_behind(displaced.astype(jnp.bfloat16), "rep", 1).astype(displaced.dtype),
        from_behind(updated_velocity.astype(jnp.bfloat16), "rep", 1).astype(updated_velocity.dtype),
        from_behind(updated_push.astype(jnp.bfloat16), "rep", 1).astype(updated_push.dtype),
    )
    upper_state = (
        from_behind(displaced.astype(jnp.bfloat16), "rep", -1).astype(displaced.dtype),
        from_behind(updated_velocity.astype(jnp.bfloat16), "rep", -1).astype(
            updated_velocity.dtype
        ),
        from_behind(updated_push.astype(jnp.bfloat16), "rep", -1).astype(updated_push.dtype),
    )
    final_pos, selected_velocity, final_force = pick_partner(
        (displaced, updated_velocity, updated_push),
        lower_state,
        upper_state,
        swap_counterpart,
        thermal_copy_entry,
    )
    closing_velocity = selected_velocity * thermal_quotient
    return (final_pos[None], closing_velocity[None], final_force[None])


def solution(mesh):
    in_specs = (
        P("rep", None, "dom"),
        P("rep", None, "dom"),
        P("rep", None, "dom"),
        P("rep", "dom"),
        P("rep", "dom"),
        P("rep", "dom", None),
        P("rep", "dom"),
        P(),
        P(),
        P(),
        P(),
        P(),
        P(),
        P(),
        P(),
        P(),
        P(),
    )
    out_specs = (P("rep", None, "dom"), P("rep", None, "dom"), P("rep", None, "dom"))
    return jax.shard_map(local, mesh=mesh, in_specs=in_specs, out_specs=out_specs, check_vma=False)
```

profile of v0, /device:TPU:280, one launch (start us, length us, event | category | flops | bytes accessed | tf_op | source)
XLA Modules:
  0.0 170.6 jit_solution(14509908160026253160)
XLA Ops:
  2.4 0.9 copy.143
  4.6 1.6 gather_fusion
  6.4 4.6 %collective-permute-start.2 = (f32[3,384]{1,0:T(4,128)S(1)}, f32[3,384]{1,0:T(4,128)S(1)}, u32[]{:S(2)}, u32[]{:S(2)}) collective-permute-start(f32[3,384]{1,0:T(4,128)S(1)} %get-tuple-element.323), channel_id=1, source_target_pairs={{0,1},{1,2},{2,3},{3,4},{4,5},{5,6},{6,7},{7,0},{8,9},{9,10},{10,1... | collective-permute-start | bytes 13832 | tf_op jit(solution)/shard_map/ppermute | solution.py:26
  11.0 1.9 %collective-permute-start.3 = (f32[3,384]{1,0:T(4,128)S(1)}, f32[3,384]{1,0:T(4,128)S(1)}, u32[]{:S(2)}, u32[]{:S(2)}) collective-permute-start(f32[3,384]{1,0:T(4,128)S(1)} %get-tuple-element.324), channel_id=1, source_target_pairs={{1,0},{2,1},{3,2},{4,3},{5,4},{6,5},{7,6},{0,7},{9,8},{10,9},{11,1... | collective-permute-start | bytes 13832 | tf_op jit(solution)/shard_map/ppermute | solution.py:28
  13.3 1.9 %gather_fusion.2 = bf16[768,128]{1,0:T(8,128)(2,1)S(1)} fusion(bf16[1024,128]{1,0:T(8,128)(2,1)S(1)} %convolution_convert_fusion.1, s32[1024]{0:T(1024)S(1)} %pad_clamp_fusion.1), kind=kCustom, calls=%fused_computation.clone | custom fusion | bytes 396288 | tf_op jit(solution)/shard_map/jit(_take)/gather | solution.py:159
  15.4 7.5 %collective-permute-start.4 = (bf16[384,128]{1,0:T(8,128)(2,1)S(1)}, bf16[384,128]{1,0:T(8,128)(2,1)S(1)}, u32[]{:S(2)}, u32[]{:S(2)}) collective-permute-start(bf16[384,128]{1,0:T(8,128)(2,1)S(1)} %get-tuple-element.321), channel_id=1, source_target_pairs={{0,1},{1,2},{2,3},{3,4},{4,5},{5,6},{6,7},{7,0},{8,9},{9,10},{10,1... | collective-permute-start | bytes 294920 | tf_op jit(solution)/shard_map/ppermute | solution.py:26
  23.0 1.9 %collective-permute-start.5 = (bf16[384,128]{1,0:T(8,128)(2,1)S(1)}, bf16[384,128]{1,0:T(8,128)(2,1)S(1)}, u32[]{:S(2)}, u32[]{:S(2)}) collective-permute-start(bf16[384,128]{1,0:T(8,128)(2,1)S(1)} %get-tuple-element.322), channel_id=1, source_target_pairs={{1,0},{2,1},{3,2},{4,3},{5,4},{6,5},{7,6},{0,7},{9,8},{10,9},{11,1... | collective-permute-start | bytes 294920 | tf_op jit(solution)/shard_map/ppermute | solution.py:28
  26.6 6.5 %collective-permute-done.5 = bf16[384,128]{1,0:T(8,128)(2,1)S(1)} collective-permute-done((bf16[384,128]{1,0:T(8,128)(2,1)S(1)}, bf16[384,128]{1,0:T(8,128)(2,1)S(1)}, u32[]{:S(2)}, u32[]{:S(2)}) %collective-permute-start.5) | collective-permute-done | bytes 98336 | tf_op jit(solution)/shard_map/ppermute | solution.py:28
  33.9 1.1 broadcast_select_fusion.1
  35.1 15.8 %while.30 = (s32[]{:T(128)}, f32[8,128,128]{2,1,0:T(8,128)S(1)}, f32[8,3,4,128]{3,2,1,0:T(4,128)S(1)}, f32[8,3,128]{2,1,0:T(4,128)S(1)}, f32[8,4]{1,0:T(8,128)S(...) while((s32[]{:T(128)}, f32[8,128,128]{2,1,0:T(8,128)S(1)}, ...), condition=%wide.region_3.6_spmd, body=%wide.region_1.5_spmd.sunk | while | flops 138133520 | bytes 1404117 | solution.py:91
  35.4 1.6 fusion.102
  37.3 1.6 fusion.102
  39.3 1.6 fusion.102
  41.3 1.6 fusion.102
  43.2 1.6 fusion.102
  45.2 1.6 fusion.102
  47.2 1.6 fusion.102
  49.2 1.6 fusion.102
  51.9 1.9 %gather_fusion.4 = bf16[768,128]{1,0:T(8,128)(2,1)S(1)} fusion(bf16[1024,128]{1,0:T(8,128)(2,1)S(1)} %fusion.45, s32[1024]{0:T(1024)S(1)} %pad_clamp_fusion.1), kind=kCustom, calls=%fused_computation.2.clone | custom fusion | bytes 396288 | tf_op jit(solution)/shard_map/jit(_take)/gather | solution.py:165
  54.0 1.9 %collective-permute-start.6 = (bf16[384,128]{1,0:T(8,128)(2,1)S(1)}, bf16[384,128]{1,0:T(8,128)(2,1)S(1)}, u32[]{:S(2)}, u32[]{:S(2)}) collective-permute-start(bf16[384,128]{1,0:T(8,128)(2,1)S(1)} %get-tuple-element.319), channel_id=1, source_target_pairs={{0,1},{1,2},{2,3},{3,4},{4,5},{5,6},{6,7},{7,0},{8,9},{9,10},{10,1... | collective-permute-start | bytes 294920 | tf_op jit(solution)/shard_map/ppermute | solution.py:26
  55.9 3.9 %collective-permute-start.7 = (bf16[384,128]{1,0:T(8,128)(2,1)S(1)}, bf16[384,128]{1,0:T(8,128)(2,1)S(1)}, u32[]{:S(2)}, u32[]{:S(2)}) collective-permute-start(bf16[384,128]{1,0:T(8,128)(2,1)S(1)} %get-tuple-element.320), channel_id=1, source_target_pairs={{1,0},{2,1},{3,2},{4,3},{5,4},{6,5},{7,6},{0,7},{9,8},{10,9},{11,1... | collective-permute-start | bytes 294920 | tf_op jit(solution)/shard_map/ppermute | solution.py:28
  60.5 5.5 %collective-permute-done.7 = bf16[384,128]{1,0:T(8,128)(2,1)S(1)} collective-permute-done((bf16[384,128]{1,0:T(8,128)(2,1)S(1)}, bf16[384,128]{1,0:T(8,128)(2,1)S(1)}, u32[]{:S(2)}, u32[]{:S(2)}) %collective-permute-start.7) | collective-permute-done | bytes 98336 | tf_op jit(solution)/shard_map/ppermute | solution.py:28
  66.1 1.7 gather_fusion.5
  67.7 2.4 %broadcast_select_fusion = bf16[8,4,128,128]{3,2,1,0:T(8,128)(2,1)} fusion(bf16[8,4,128,128]{3,2,1,0:T(8,128)(2,1)} %bitcast.244, pred[8,4]{1,0:T(8,128)(4,1)S(1)} %copy.144), kind=kLoop, calls=%fused_computation.82 | loop fusion | flops 524288 | bytes 2097184 | tf_op jit(solution)/shard_map/jit(_take)/select_n | solution.py:81
  70.1 15.8 %while.31 = (s32[]{:T(128)}, f32[8,128,128]{2,1,0:T(8,128)S(1)}, f32[8,3,4,128]{3,2,1,0:T(4,128)S(1)}, f32[8,3,128]{2,1,0:T(4,128)S(1)}, f32[8,4]{1,0:T(8,128)S(...) while((s32[]{:T(128)}, f32[8,128,128]{2,1,0:T(8,128)S(1)}, ...), condition=%wide.region_7.10_spmd, body=%wide.region_5.9_spmd.sunk | while | flops 138133520 | bytes 1404117 | solution.py:91
  70.4 1.6 fusion.106
  72.4 1.6 fusion.106
  74.4 1.6 fusion.106
  76.4 1.6 fusion.106
  78.3 1.6 fusion.106
  80.3 1.6 fusion.106
  82.3 1.6 fusion.106
  84.2 1.6 fusion.106
  86.6 1.9 %gather_fusion.6 = bf16[768,128]{1,0:T(8,128)(2,1)S(1)} fusion(bf16[1024,128]{1,0:T(8,128)(2,1)S(1)} %fusion.46, s32[1024]{0:T(1024)S(1)} %pad_clamp_fusion.1), kind=kCustom, calls=%fused_computation.3.clone | custom fusion | bytes 396288 | tf_op jit(solution)/shard_map/jit(_take)/gather | solution.py:174
  88.7 1.9 %collective-permute-start.8 = (bf16[384,128]{1,0:T(8,128)(2,1)S(1)}, bf16[384,128]{1,0:T(8,128)(2,1)S(1)}, u32[]{:S(2)}, u32[]{:S(2)}) collective-permute-start(bf16[384,128]{1,0:T(8,128)(2,1)S(1)} %get-tuple-element.317), channel_id=1, source_target_pairs={{0,1},{1,2},{2,3},{3,4},{4,5},{5,6},{6,7},{7,0},{8,9},{9,10},{10,1... | collective-permute-start | bytes 294920 | tf_op jit(solution)/shard_map/ppermute | solution.py:26
  90.6 3.9 %collective-permute-start.9 = (bf16[384,128]{1,0:T(8,128)(2,1)S(1)}, bf16[384,128]{1,0:T(8,128)(2,1)S(1)}, u32[]{:S(2)}, u32[]{:S(2)}) collective-permute-start(bf16[384,128]{1,0:T(8,128)(2,1)S(1)} %get-tuple-element.318), channel_id=1, source_target_pairs={{1,0},{2,1},{3,2},{4,3},{5,4},{6,5},{7,6},{0,7},{9,8},{10,9},{11,1... | collective-permute-start | bytes 294920 | tf_op jit(solution)/shard_map/ppermute | solution.py:28
  95.2 5.5 %collective-permute-done.9 = bf16[384,128]{1,0:T(8,128)(2,1)S(1)} collective-permute-done((bf16[384,128]{1,0:T(8,128)(2,1)S(1)}, bf16[384,128]{1,0:T(8,128)(2,1)S(1)}, u32[]{:S(2)}, u32[]{:S(2)}) %collective-permute-start.9) | collective-permute-done | bytes 98336 | tf_op jit(solution)/shard_map/ppermute | solution.py:28
  101.8 1.1 broadcast_select_fusion.2
  102.9 29.9 %while.32 = (s32[]{:T(128)}, f32[8,3,128]{2,1,0:T(4,128)S(1)}, f32[8,3,4,128]{3,1,2,0:T(4,128)S(1)}, bf16[8,4,128,128]{3,2,1,0:T(8,128)(2,1)}, bf16[8,128,128]{2...) while((s32[]{:T(128)}, f32[8,3,128]{2,1,0:T(4,128)S(1)}, ...), condition=%wide.region_12.15_spmd, body=%wide.region_9.14_spmd.sunk | while | flops 29295240 | bytes 4933369 | solution.py:127
  103.8 1.3 fusion.112
  105.2 1.2 fusion.113
  107.6 1.3 fusion.112
  109.0 1.2 fusion.113
  111.3 1.3 fusion.112
  112.7 1.2 fusion.113
  115.0 1.3 fusion.112
  116.5 1.2 fusion.113
  118.8 1.3 fusion.112
  120.2 1.2 fusion.113
  122.5 1.3 fusion.112
  123.9 1.1 fusion.113
  126.3 1.3 fusion.112
  127.7 1.1 fusion.113
  130.0 1.3 fusion.112
  131.4 1.2 fusion.113
  133.1 1.9 %collective-permute-start.12 = (bf16[3,1024]{0,1:T(8,128)(2,1)S(1)}, bf16[3,1024]{0,1:T(8,128)(2,1)S(1)}, u32[]{:S(2)}, u32[]{:S(2)}) collective-permute-start(bf16[3,1024]{0,1:T(8,128)(2,1)S(1)} %bitcast_convert_fusion), channel_id=1, source_target_pairs={{8,0},{16,8},{24,16},{32,24},{40,32},{48,40},{56,48},{64,56},{72,6... | collective-permute-start | bytes 18440 | tf_op jit(solution)/shard_map/ppermute | solution.py:38
  135.0 2.4 %collective-permute-start.13 = (bf16[3,1024]{0,1:T(8,128)(2,1)S(1)}, bf16[3,1024]{0,1:T(8,128)(2,1)S(1)}, u32[]{:S(2)}, u32[]{:S(2)}) collective-permute-start(bf16[3,1024]{0,1:T(8,128)(2,1)S(1)} %bitcast_convert_fusion), channel_id=1, source_target_pairs={{0,8},{8,16},{16,24},{24,32},{32,40},{40,48},{48,56},{56,64},{64,7... | collective-permute-start | bytes 18440 | tf_op jit(solution)/shard_map/ppermute | solution.py:38
  137.5 5.3 %collective-permute-start = (bf16[3,1024]{0,1:T(8,128)(2,1)S(1)}, bf16[3,1024]{0,1:T(8,128)(2,1)}, u32[]{:S(2)}, u32[]{:S(2)}) collective-permute-start(bf16[3,1024]{0,1:T(8,128)(2,1)S(1)} %copy-done.1), channel_id=1, source_target_pairs={{8,0},{16,8},{24,16},{32,24},{40,32},{48,40},{56,48},{64,56},{72,6... | collective-permute-start | bytes 18440 | tf_op jit(solution)/shard_map/ppermute | solution.py:38
  142.7 1.9 %collective-permute-start.1 = (bf16[3,1024]{0,1:T(8,128)(2,1)S(1)}, bf16[3,1024]{0,1:T(8,128)(2,1)}, u32[]{:S(2)}, u32[]{:S(2)}) collective-permute-start(bf16[3,1024]{0,1:T(8,128)(2,1)S(1)} %copy-done.1), channel_id=1, source_target_pairs={{0,8},{8,16},{16,24},{24,32},{32,40},{40,48},{48,56},{56,64},{64,7... | collective-permute-start | bytes 18440 | tf_op jit(solution)/shard_map/ppermute | solution.py:38
  151.9 2.0 %fusion.66 = (bf16[3,1024]{0,1:T(8,128)(2,1)}, f32[3,1024]{0,1:T(8,128)S(1)}, f32[3,1024]{0,1:T(8,128)S(1)}) fusion(f32[3,8,128]{0,2,1:T(8,128)S(1)} %copy.159, f32[1024]{0:T(1024)S(1)} %get-tuple-element.327, f32[1,3,1024]{1,2,0:T(8,128)S(1)} %copy.143, f32[1,3,1024]{1,2,0:T(8,128)S(1)} %copy.142, bf16[3,1024]{0,1:T(8,128)(2,1)} %copy-done.3, pred[]{:T(512)S(6)} %eq.46, ...), kind=kLoop, calls=%fused_computation.151 | loop fusion | flops 27648 | bytes 83970 | tf_op jit(solution)/shard_map/convert_element_type | solution.py:255
  153.9 5.7 %collective-permute-start.10 = (bf16[3,1024]{0,1:T(8,128)(2,1)}, bf16[3,1024]{0,1:T(8,128)(2,1)S(1)}, u32[]{:S(2)}, u32[]{:S(2)}) collective-permute-start(bf16[3,1024]{0,1:T(8,128)(2,1)} %get-tuple-element.310), channel_id=1, source_target_pairs={{8,0},{16,8},{24,16},{32,24},{40,32},{48,40},{56,48},{64,56},{72,6... | collective-permute-start | bytes 18440 | tf_op jit(solution)/shard_map/ppermute | solution.py:38
  159.7 1.9 %collective-permute-start.11 = (bf16[3,1024]{0,1:T(8,128)(2,1)}, bf16[3,1024]{0,1:T(8,128)(2,1)S(1)}, u32[]{:S(2)}, u32[]{:S(2)}) collective-permute-start(bf16[3,1024]{0,1:T(8,128)(2,1)} %get-tuple-element.310), channel_id=1, source_target_pairs={{0,8},{8,16},{16,24},{24,32},{32,40},{40,48},{48,56},{56,64},{64,7... | collective-permute-start | bytes 18440 | tf_op jit(solution)/shard_map/ppermute | solution.py:38
  161.6 1.1 select_bitcast_fusion
  164.3 5.4 %collective-permute-done.11 = bf16[3,1024]{0,1:T(8,128)(2,1)S(1)} collective-permute-done((bf16[3,1024]{0,1:T(8,128)(2,1)}, bf16[3,1024]{0,1:T(8,128)(2,1)S(1)}, u32[]{:S(2)}, u32[]{:S(2)}) %collective-permute-start.11) | collective-permute-done | bytes 6176 | tf_op jit(solution)/shard_map/ppermute | solution.py:38
  (309 shorter events, 29.6 us)
Async XLA Ops:
  0.6 100.1 %copy-start = (bf16[128,128]{1,0:T(8,128)(2,1)S(1)}, bf16[128,128]{1,0:T(8,128)(2,1)}, u32[]{:S(2)}) copy-start(bf16[128,128]{1,0:T(8,128)(2,1)} %param.40) | copy-start | bytes 98308
  0.6 2.7 %copy-start.6 = (f32[1,3,1024]{2,0,1:T(1,128)S(1)}, f32[1,3,1024]{2,0,1:T(1,128)}, u32[]{:S(2)}) copy-start(f32[1,3,1024]{2,0,1:T(1,128)} %param.27) | copy-start | bytes 36868
  0.7 2.9 %copy-start.12 = (s32[1,768]{1,0:T(1,128)S(1)}, s32[1,768]{1,0:T(1,128)}, u32[]{:S(2)}) copy-start(s32[1,768]{1,0:T(1,128)} %param.31) | copy-start | bytes 9220
  3.6 9.3 %copy-start.10 = (s32[1,1024]{1,0:T(1,128)S(1)}, s32[1,1024]{1,0:T(1,128)}, u32[]{:S(2)}) copy-start(s32[1,1024]{1,0:T(1,128)} %param.30) | copy-start | bytes 12292
  3.6 9.3 %copy-start.14 = (bf16[16,128]{1,0:T(8,128)(2,1)S(1)}, bf16[16,128]{1,0:T(8,128)(2,1)}, u32[]{:S(2)}) copy-start(bf16[16,128]{1,0:T(8,128)(2,1)} %param.34) | copy-start | bytes 12292
  6.4 19.4 %collective-permute-start.2 = (f32[3,384]{1,0:T(4,128)S(1)}, f32[3,384]{1,0:T(4,128)S(1)}, u32[]{:S(2)}, u32[]{:S(2)}) collective-permute-start(f32[3,384]{1,0:T(4,128)S(1)} %get-tuple-element.323), channel_id=1, source_target_pairs={{0,1},{1,2},{2,3},{3,4},{4,5},{5,6},{6,7},{7,0},{8,9},{9,10},{10,1... | collective-permute-start | bytes 13832 | tf_op jit(solution)/shard_map/ppermute | solution.py:26
  11.0 14.8 %collective-permute-start.3 = (f32[3,384]{1,0:T(4,128)S(1)}, f32[3,384]{1,0:T(4,128)S(1)}, u32[]{:S(2)}, u32[]{:S(2)}) collective-permute-start(f32[3,384]{1,0:T(4,128)S(1)} %get-tuple-element.324), channel_id=1, source_target_pairs={{1,0},{2,1},{3,2},{4,3},{5,4},{6,5},{7,6},{0,7},{9,8},{10,9},{11,1... | collective-permute-start | bytes 13832 | tf_op jit(solution)/shard_map/ppermute | solution.py:28
  13.3 11.6 %copy-start.9 = (s32[1,8,4]{1,2,0:T(4,128)S(1)}, s32[1,8,4]{1,2,0:T(4,128)}, u32[]{:S(2)}) copy-start(s32[1,8,4]{1,2,0:T(4,128)} %param.32) | copy-start | bytes 388
  13.3 11.7 %copy-start.5 = (f32[1,3,1024]{2,0,1:T(1,128)S(1)}, f32[1,3,1024]{2,0,1:T(1,128)}, u32[]{:S(2)}) copy-start(f32[1,3,1024]{2,0,1:T(1,128)} %param.28) | copy-start | bytes 36868
  13.3 12.0 %copy-start.17 = (s32[1,8]{1,0:T(1,128)S(1)}, s32[1,8]{1,0:T(1,128)}, u32[]{:S(2)}) copy-start(s32[1,8]{1,0:T(1,128)} %param.33) | copy-start | bytes 100
  13.3 12.1 %copy-start.13 = (f32[2,8,128]{2,1,0:T(8,128)S(1)}, f32[2,8,128]{2,1,0:T(8,128)}, u32[]{:S(2)}) copy-start(f32[2,8,128]{2,1,0:T(8,128)} %param.36) | copy-start | bytes 24580
  13.3 12.1 %copy-start.16 = (f32[2,128]{1,0:T(2,128)S(1)}, f32[2,128]{1,0:T(2,128)}, u32[]{:S(2)}) copy-start(f32[2,128]{1,0:T(2,128)} %param.37) | copy-start | bytes 3076
  13.3 12.1 %copy-start.7 = (f32[1,3,1024]{2,0,1:T(1,128)S(1)}, f32[1,3,1024]{2,0,1:T(1,128)}, u32[]{:S(2)}) copy-start(f32[1,3,1024]{2,0,1:T(1,128)} %param.29) | copy-start | bytes 36868
  15.4 11.2 %collective-permute-start.4 = (bf16[384,128]{1,0:T(8,128)(2,1)S(1)}, bf16[384,128]{1,0:T(8,128)(2,1)S(1)}, u32[]{:S(2)}, u32[]{:S(2)}) collective-permute-start(bf16[384,128]{1,0:T(8,128)(2,1)S(1)} %get-tuple-element.321), channel_id=1, source_target_pairs={{0,1},{1,2},{2,3},{3,4},{4,5},{5,6},{6,7},{7,0},{8,9},{9,10},{10,1... | collective-permute-start | bytes 294920 | tf_op jit(solution)/shard_map/ppermute | solution.py:26
  23.0 10.1 %collective-permute-start.5 = (bf16[384,128]{1,0:T(8,128)(2,1)S(1)}, bf16[384,128]{1,0:T(8,128)(2,1)S(1)}, u32[]{:S(2)}, u32[]{:S(2)}) collective-permute-start(bf16[384,128]{1,0:T(8,128)(2,1)S(1)} %get-tuple-element.322), channel_id=1, source_target_pairs={{1,0},{2,1},{3,2},{4,3},{5,4},{6,5},{7,6},{0,7},{9,8},{10,9},{11,1... | collective-permute-start | bytes 294920 | tf_op jit(solution)/shard_map/ppermute | solution.py:28
  50.8 0.8 copy-start.4
  54.0 6.5 %collective-permute-start.6 = (bf16[384,128]{1,0:T(8,128)(2,1)S(1)}, bf16[384,128]{1,0:T(8,128)(2,1)S(1)}, u32[]{:S(2)}, u32[]{:S(2)}) collective-permute-start(bf16[384,128]{1,0:T(8,128)(2,1)S(1)} %get-tuple-element.319), channel_id=1, source_target_pairs={{0,1},{1,2},{2,3},{3,4},{4,5},{5,6},{6,7},{7,0},{8,9},{9,10},{10,1... | collective-permute-start | bytes 294920 | tf_op jit(solution)/shard_map/ppermute | solution.py:26
  55.9 10.1 %collective-permute-start.7 = (bf16[384,128]{1,0:T(8,128)(2,1)S(1)}, bf16[384,128]{1,0:T(8,128)(2,1)S(1)}, u32[]{:S(2)}, u32[]{:S(2)}) collective-permute-start(bf16[384,128]{1,0:T(8,128)(2,1)S(1)} %get-tuple-element.320), channel_id=1, source_target_pairs={{1,0},{2,1},{3,2},{4,3},{5,4},{6,5},{7,6},{0,7},{9,8},{10,9},{11,1... | collective-permute-start | bytes 294920 | tf_op jit(solution)/shard_map/ppermute | solution.py:28
  86.6 8.0 %copy-start.8 = (bf16[128,128]{1,0:T(8,128)(2,1)S(1)}, bf16[128,128]{1,0:T(8,128)(2,1)}, u32[]{:S(2)}) copy-start(bf16[128,128]{1,0:T(8,128)(2,1)} %param.39) | copy-start | bytes 98308
  88.7 6.5 %collective-permute-start.8 = (bf16[384,128]{1,0:T(8,128)(2,1)S(1)}, bf16[384,128]{1,0:T(8,128)(2,1)S(1)}, u32[]{:S(2)}, u32[]{:S(2)}) collective-permute-start(bf16[384,128]{1,0:T(8,128)(2,1)S(1)} %get-tuple-element.317), channel_id=1, source_target_pairs={{0,1},{1,2},{2,3},{3,4},{4,5},{5,6},{6,7},{7,0},{8,9},{9,10},{10,1... | collective-permute-start | bytes 294920 | tf_op jit(solution)/shard_map/ppermute | solution.py:26
  90.6 10.1 %collective-permute-start.9 = (bf16[384,128]{1,0:T(8,128)(2,1)S(1)}, bf16[384,128]{1,0:T(8,128)(2,1)S(1)}, u32[]{:S(2)}, u32[]{:S(2)}) collective-permute-start(bf16[384,128]{1,0:T(8,128)(2,1)S(1)} %get-tuple-element.318), channel_id=1, source_target_pairs={{1,0},{2,1},{3,2},{4,3},{5,4},{6,5},{7,6},{0,7},{9,8},{10,9},{11,1... | collective-permute-start | bytes 294920 | tf_op jit(solution)/shard_map/ppermute | solution.py:28
  101.8 1.2 copy-start.11
  132.8 4.6 %copy-start.1 = (bf16[3,1024]{0,1:T(8,128)(2,1)S(1)}, bf16[3,1024]{0,1:T(8,128)(2,1)}, u32[]{:S(2)}) copy-start(bf16[3,1024]{0,1:T(8,128)(2,1)} %get-tuple-element.312) | copy-start | bytes 18436
  132.8 11.9 %copy-start.18 = (s32[64]{0:T(128)S(1)}, s32[64]{0:T(128)}, u32[]{:S(2)}) copy-start(s32[64]{0:T(128)} %param.43) | copy-start | bytes 772
  132.8 15.7 %copy-start.15 = (f32[64]{0:T(128)S(1)}, f32[64]{0:T(128)}, u32[]{:S(2)}) copy-start(f32[64]{0:T(128)} %param.42) | copy-start | bytes 772
  133.1 17.4 %collective-permute-start.12 = (bf16[3,1024]{0,1:T(8,128)(2,1)S(1)}, bf16[3,1024]{0,1:T(8,128)(2,1)S(1)}, u32[]{:S(2)}, u32[]{:S(2)}) collective-permute-start(bf16[3,1024]{0,1:T(8,128)(2,1)S(1)} %bitcast_convert_fusion), channel_id=1, source_target_pairs={{8,0},{16,8},{24,16},{32,24},{40,32},{48,40},{56,48},{64,56},{72,6... | collective-permute-start | bytes 18440 | tf_op jit(solution)/shard_map/ppermute | solution.py:38
  135.0 15.5 %collective-permute-start.13 = (bf16[3,1024]{0,1:T(8,128)(2,1)S(1)}, bf16[3,1024]{0,1:T(8,128)(2,1)S(1)}, u32[]{:S(2)}, u32[]{:S(2)}) collective-permute-start(bf16[3,1024]{0,1:T(8,128)(2,1)S(1)} %bitcast_convert_fusion), channel_id=1, source_target_pairs={{0,8},{8,16},{16,24},{24,32},{32,40},{40,48},{48,56},{56,64},{64,7... | collective-permute-start | bytes 18440 | tf_op jit(solution)/shard_map/ppermute | solution.py:38
  137.5 24.2 %collective-permute-start = (bf16[3,1024]{0,1:T(8,128)(2,1)S(1)}, bf16[3,1024]{0,1:T(8,128)(2,1)}, u32[]{:S(2)}, u32[]{:S(2)}) collective-permute-start(bf16[3,1024]{0,1:T(8,128)(2,1)S(1)} %copy-done.1), channel_id=1, source_target_pairs={{8,0},{16,8},{24,16},{32,24},{40,32},{48,40},{56,48},{64,56},{72,6... | collective-permute-start | bytes 18440 | tf_op jit(solution)/shard_map/ppermute | solution.py:38
  142.7 18.9 %collective-permute-start.1 = (bf16[3,1024]{0,1:T(8,128)(2,1)S(1)}, bf16[3,1024]{0,1:T(8,128)(2,1)}, u32[]{:S(2)}, u32[]{:S(2)}) collective-permute-start(bf16[3,1024]{0,1:T(8,128)(2,1)S(1)} %copy-done.1), channel_id=1, source_target_pairs={{0,8},{8,16},{16,24},{24,32},{32,40},{40,48},{48,56},{56,64},{64,7... | collective-permute-start | bytes 18440 | tf_op jit(solution)/shard_map/ppermute | solution.py:38
  150.5 0.7 copy-start.2
  151.2 0.7 copy-start.3
  153.9 10.4 %collective-permute-start.10 = (bf16[3,1024]{0,1:T(8,128)(2,1)}, bf16[3,1024]{0,1:T(8,128)(2,1)S(1)}, u32[]{:S(2)}, u32[]{:S(2)}) collective-permute-start(bf16[3,1024]{0,1:T(8,128)(2,1)} %get-tuple-element.310), channel_id=1, source_target_pairs={{8,0},{16,8},{24,16},{32,24},{40,32},{48,40},{56,48},{64,56},{72,6... | collective-permute-start | bytes 18440 | tf_op jit(solution)/shard_map/ppermute | solution.py:38
  159.7 10.0 %collective-permute-start.11 = (bf16[3,1024]{0,1:T(8,128)(2,1)}, bf16[3,1024]{0,1:T(8,128)(2,1)S(1)}, u32[]{:S(2)}, u32[]{:S(2)}) collective-permute-start(bf16[3,1024]{0,1:T(8,128)(2,1)} %get-tuple-element.310), channel_id=1, source_target_pairs={{0,8},{8,16},{16,24},{24,32},{32,40},{40,48},{48,56},{56,64},{64,7... | collective-permute-start | bytes 18440 | tf_op jit(solution)/shard_map/ppermute | solution.py:38
where the time goes:
time: 172 us; the launch traced here: 171 us
  matrix products  48.8 us (28%)
  starting transfers between devices  46.8 us (27%)
  waiting for transfers between devices  24 us (14%)
  local copies, waits for them, and re-layouts  23 us (13%)
  other arithmetic  19.9 us (12%)
  between operations  6.07 us (4%)
  loops' own time  1.87 us (1%)
    dot_general x16, matrix products, one_tile(): jnp.einsum('kbij,kjc->bic', basis_val, far_feat, preferred_element_type=j...  26.3 us
    ppermute x6, starting transfers between devices, from_behind(): return lax.ppermute(array, axis, pairs)  19.2 us
    ppermute x4, waiting for transfers between devices, with_halo(): lax.ppermute(head, axis, [((i + 1) % count, i) for i in range(count)])  17.6 us
    ppermute x4, starting transfers between devices, with_halo(): lax.ppermute(tail, axis, [(i, (i + 1) % count) for i in range(count)])  16 us
    ppermute x4, starting transfers between devices, with_halo(): lax.ppermute(head, axis, [((i + 1) % count, i) for i in range(count)])  11.7 us
    dot_general x8, matrix products, one_tile(): jnp.einsum('kbij,b->kij', basis_val.astype(jnp.float32), push_distance_ta...  10.2 us
    dot_general x8, matrix products, one_tile(): jnp.einsum('ic,kjc->kij', asking, far_keys, preferred_element_type=jnp.fl...  9.2 us
    unnamed x44, local copies, waits for them, and re-layouts  6.32 us
  transfers between devices with their start and end apart: 14, of which 6 were waited for; matrix products, arithmetic and copies ran while one was open for 6% of the time, Pallas kernels for 0%

commit v1 on v0

v1 whole, which is shorter than its diff:
```python
import math

import jax
import jax.numpy as jnp
from jax import lax
from jax.experimental import pallas as pl
from jax.experimental.pallas import tpu as pltpu
from jax.sharding import PartitionSpec as P

NB = 8
TILE = 128
NEI = 4
TILES = 8
GT = 3
EXT = TILES + 2 * GT
ATOMS = TILES * TILE
SPECIES = 16
CH = 128
CHUNK = 32

slab_width = 1.5
time_step = 0.5
basis_width = 0.3
norm_eps = 1e-06
factor = 1.0 / math.sqrt(CH * NEI * TILE)

ROOT = math.sqrt(math.log2(math.e))
SCALE = ROOT / basis_width
TOP = (NB - 1) * ROOT
FAR = 1.0e3

MESH = pl.DeviceIdType.MESH


def columns(row):
    return jnp.broadcast_to(row, (TILE, TILE)).T


def pick(offset, own, low, high):
    return jnp.where(offset == 1, high, jnp.where(offset == -1, low, own))


def step_kernel(
    reps,
    doms,
    loc_ref,
    spd_ref,
    frc_ref,
    kind_ref,
    ghost_ref,
    adj_ref,
    live_ref,
    vec_ref,
    inertia_ref,
    radial_ref,
    gain_ref,
    mix_ref,
    target_ref,
    source_ref,
    taper_ref,
    heat_ref,
    swap_ref,
    pos_out,
    vel_out,
    frc_out,
    posext,
    psend,
    xcol,
    hext,
    mid,
    keys,
    hsend,
    onehot,
    basis,
    env,
    hcat,
    scores,
    facc,
    last,
    query,
    state,
    state_in,
    fown,
    f_in,
    send_sem,
    recv_sem,
):
    rep = lax.axis_index("rep")
    dom = lax.axis_index("dom")
    rep_to = (lax.rem(rep + 1, reps), lax.rem(rep + reps - 1, reps))
    dom_to = (lax.rem(dom + 1, doms), lax.rem(dom + doms - 1, doms))

    barrier = pltpu.get_barrier_semaphore()
    for side in range(2):
        pl.semaphore_signal(barrier, inc=1, device_id={"dom": dom_to[side]}, device_id_type=MESH)
        pl.semaphore_signal(barrier, inc=1, device_id={"rep": rep_to[side]}, device_id_type=MESH)

    def copy(stage, side, axis, src, dst):
        to = dom_to[side] if axis == "dom" else rep_to[side]
        return pltpu.make_async_remote_copy(
            src_ref=src,
            dst_ref=dst,
            send_sem=send_sem.at[2 * stage + side],
            recv_sem=recv_sem.at[2 * stage + side],
            device_id={axis: to},
            device_id_type=MESH,
        )

    kinds = kind_ref[...]
    mass = jnp.zeros((1, ATOMS), jnp.float32)
    for s in range(SPECIES):
        mass = jnp.where(kinds == s, inertia_ref[s], mass)
    inv_mass = 1.0 / mass
    loc, spd, frc = loc_ref[0], spd_ref[0], frc_ref[0]
    moved = loc + time_step * spd + 0.5 * time_step * time_step * frc * inv_mass
    half = spd + 0.5 * time_step * frc * inv_mass
    kindf = kinds.astype(jnp.float32)
    for t in range(TILES):
        lanes = slice(t * TILE, (t + 1) * TILE)
        posext[t] = jnp.zeros((8, TILE), jnp.float32)
        posext[t, 0:3, :] = moved[:, lanes]
        posext[t, 3:4, :] = kindf[:, lanes]

    first_row = lax.broadcasted_iota(jnp.int32, (8, TILE), 0) == 0
    for side in range(2):
        for g in range(GT):
            start = ((1 - side) * GT + g) * TILE
            label = jnp.broadcast_to(ghost_ref[:, start : start + TILE], (8, TILE))
            place = label & (TILE - 1)
            owner = label >> 7
            out = jnp.zeros((8, TILE), jnp.float32)
            for t in range(TILES):
                got = jnp.take_along_axis(posext[t], place, axis=1, mode="promise_in_bounds")
                out = jnp.where(owner == t, got, out)
            shift = slab_width if side == 1 else -slab_width
            psend[side, g] = jnp.where(first_row, out + shift, out)

    pl.semaphore_wait(barrier, 4)
    pos_copies = [
        copy(0, side, "dom", psend.at[side], posext.at[pl.ds(TILES + GT * side, GT)])
        for side in range(2)
    ]
    for c in pos_copies:
        c.start()

    state[0:3, :] = moved
    state[3:6, :] = half
    state[6:7, :] = inv_mass
    state[7:8, :] = inv_mass
    state_copies = [copy(1, side, "rep", state, state_in.at[side]) for side in range(2)]
    for c in state_copies:
        c.start()

    lane = lax.broadcasted_iota(jnp.int32, (TILE, TILE), 1)
    lanef = lane.astype(jnp.float32)
    vectors = jnp.concatenate([vec_ref[...], jnp.zeros((TILE - SPECIES, CH), jnp.bfloat16)], axis=0)

    def embed(s):
        hot = jnp.where(columns(posext[s, 3:4, :]) == lanef, 1.0, 0.0).astype(jnp.bfloat16)
        hext[s] = jnp.dot(hot, vectors, preferred_element_type=jnp.float32).astype(jnp.bfloat16)

    def own_tile(t, _):
        for axis in range(3):
            xcol[t, axis] = columns(posext[t, axis : axis + 1, :])
        embed(t)
        return 0

    lax.fori_loop(0, TILES, own_tile, 0)

    for g in range(2 * GT):
        labels = columns(ghost_ref[:, g * TILE : (g + 1) * TILE])
        for t in range(TILES):
            hot = jnp.where(labels == lane + t * TILE, 1.0, 0.0).astype(jnp.bfloat16)
            onehot[g * TILE : (g + 1) * TILE, t * TILE : (t + 1) * TILE] = hot

    for c in pos_copies:
        c.wait()

    def ghost_tile(s, _):
        embed(s)
        return 0

    lax.fori_loop(TILES, EXT, ghost_tile, 0)

    def fill_basis(t):
        for k in range(NEI):
            far = posext[adj_ref[0, t, k]]
            dead = jnp.clip(k + 1 - live_ref[0, t], 0, 1).astype(jnp.float32) * FAR
            xj, yj, zj = far[0:1, :] + dead, far[1:2, :], far[2:3, :]
            for c in range(TILE // CHUNK):
                rows = slice(c * CHUNK, (c + 1) * CHUNK)
                dx = xj - xcol[t, 0, rows, :]
                dy = yj - xcol[t, 1, rows, :]
                dz = zj - xcol[t, 2, rows, :]
                square = dx * dx + dy * dy + dz * dz
                a = square * lax.rsqrt(jnp.maximum(square, 1e-30)) * SCALE
                top = a - TOP
                g = jnp.exp2(-(top * top))
                q = jnp.exp2(a * (-2.0 * ROOT))
                for b in range(NB - 1, -1, -1):
                    basis[t, b, rows, k * TILE : (k + 1) * TILE] = g.astype(jnp.bfloat16)
                    if b:
                        g = g * (q * math.exp(2 * b - 1))

    def layer_tile(layer, t, source):
        for k in range(NEI):
            hcat[k * TILE : (k + 1) * TILE, :] = source[adj_ref[0, t, k]]
        summed = jnp.dot(
            basis[t].reshape(NB * TILE, NEI * TILE), hcat[...], preferred_element_type=jnp.float32
        )
        radial = radial_ref[layer]
        messages = radial[0:1, :] * summed[0:TILE, :]
        for b in range(1, NB):
            messages = messages + radial[b : b + 1, :] * summed[b * TILE : (b + 1) * TILE, :]
        inverse = lax.rsqrt(jnp.mean(messages * messages, axis=-1, keepdims=True) + norm_eps)
        scaled = messages * inverse * gain_ref[layer : layer + 1, :]
        activation = (scaled / (1.0 + jnp.exp(-scaled))).astype(jnp.bfloat16)
        return (
            source[t].astype(jnp.float32)
            + jnp.dot(activation, mix_ref[layer], preferred_element_type=jnp.float32)
        ).astype(jnp.bfloat16)

    def first_layer(t, _):
        fill_basis(t)
        mid[t] = layer_tile(0, t, hext)
        return 0

    lax.fori_loop(0, TILES, first_layer, 0)

    def export(stage, rows, buffer, slot):
        copies = []
        for side in range(2):
            start = (1 - side) * GT * TILE
            packed = jnp.dot(
                onehot[start : start + GT * TILE, :], rows, preferred_element_type=jnp.float32
            )
            hsend[slot, side] = packed.astype(jnp.bfloat16).reshape(GT, TILE, CH)
            c = copy(
                stage, side, "dom", hsend.at[slot, side], buffer.at[pl.ds(TILES + GT * side, GT)]
            )
            c.start()
            copies.append(c)
        return copies

    mid_copies = export(2, mid[0:TILES].reshape(ATOMS, CH), mid, 0)

    def fill_env(t, _):
        for c in range(TILE // CHUNK):
            rows = slice(c * CHUNK, (c + 1) * CHUNK)
            total = taper_ref[0] * basis[t, 0, rows, :].astype(jnp.float32)
            for b in range(1, NB):
                total = total + taper_ref[b] * basis[t, b, rows, :].astype(jnp.float32)
            env[t, rows, :] = total * factor
        return 0

    lax.fori_loop(0, TILES, fill_env, 0)

    for c in mid_copies:
        c.wait()

    def second_layer(t, _):
        hidden = layer_tile(1, t, mid)
        last[t] = hidden
        keys[t] = jnp.dot(
            hidden, source_ref[...], preferred_element_type=jnp.float32
        ).astype(jnp.bfloat16)
        return 0

    lax.fori_loop(0, TILES, second_layer, 0)
    key_copies = export(3, keys[0:TILES].reshape(ATOMS, CH), keys, 1)

    query[...] = (
        jnp.dot(
            last[...].reshape(ATOMS, CH), target_ref[...], preferred_element_type=jnp.float32
        )
        .astype(jnp.bfloat16)
        .reshape(TILES, TILE, CH)
    )
    for c in state_copies:
        c.wait()
    partner = swap_ref[rep]
    offset = jnp.full((3, ATOMS), partner - rep, jnp.int32)
    own_state, low_state, high_state = state[...], state_in[0], state_in[1]
    pos_out[0] = pick(offset, own_state[0:3], low_state[0:3], high_state[0:3])
    half_of = pick(offset, own_state[3:6], low_state[3:6], high_state[3:6])
    inv_of = pick(offset[0:1], own_state[6:7], low_state[6:7], high_state[6:7])
    quotient = jnp.sqrt(
        jnp.full((1, ATOMS), heat_ref[rep], jnp.float32)
        / jnp.full((1, ATOMS), heat_ref[partner], jnp.float32)
    )

    for c in key_copies:
        c.wait()

    def force_tile(t, _):
        for k in range(NEI):
            hcat[k * TILE : (k + 1) * TILE, :] = keys[adj_ref[0, t, k]]
        scores[...] = lax.dot_general(
            query[t], hcat[...], (((1,), (1,)), ((), ())), preferred_element_type=jnp.float32
        )
        fars = [posext[adj_ref[0, t, k]] for k in range(NEI)]
        for c in range(TILE // CHUNK):
            rows = slice(c * CHUNK, (c + 1) * CHUNK)
            weights = scores[rows, :] * env[t, rows, :]
            for axis in range(3):
                near = xcol[t, axis, rows, :]
                total = jnp.zeros((CHUNK, TILE), jnp.float32)
                for k in range(NEI):
                    weight = weights[:, k * TILE : (k + 1) * TILE]
                    total = total + weight * (fars[k][axis : axis + 1, :] - near)
                facc[axis, rows, :] = total
        for axis in range(3):
            fown[axis : axis + 1, pl.ds(pl.multiple_of(t * TILE, TILE), TILE)] = jnp.sum(
                facc[axis].T, axis=0, keepdims=True
            )
        return 0

    lax.fori_loop(0, TILES, force_tile, 0)

    f_copies = [copy(4, side, "rep", fown, f_in.at[side]) for side in range(2)]
    for c in f_copies:
        c.start()
    for c in f_copies:
        c.wait()
    force = pick(offset, fown[...], f_in[0], f_in[1])
    frc_out[0] = force
    vel_out[0] = (half_of + 0.5 * time_step * force * inv_of) * quotient


def solution(mesh):
    reps, doms = mesh.shape["rep"], mesh.shape["dom"]

    def kernel(*refs):
        step_kernel(reps, doms, *refs)

    def local(*args):
        vmem = pl.BlockSpec(memory_space=pltpu.VMEM)
        smem = pl.BlockSpec(memory_space=pltpu.SMEM)
        out = jax.ShapeDtypeStruct((1, 3, ATOMS), jnp.float32)
        f32, bf16 = jnp.float32, jnp.bfloat16
        return pl.pallas_call(
            kernel,
            out_shape=(out, out, out),
            in_specs=[
                vmem, vmem, vmem, vmem, vmem, smem, smem, vmem, smem,
                vmem, vmem, vmem, vmem, vmem, smem, smem, smem,
            ],
            out_specs=(vmem, vmem, vmem),
            scratch_shapes=[
                pltpu.VMEM((EXT, 8, TILE), f32),
                pltpu.VMEM((2, GT, 8, TILE), f32),
                pltpu.VMEM((TILES, 3, TILE, TILE), f32),
                pltpu.VMEM((EXT, TILE, CH), bf16),
                pltpu.VMEM((EXT, TILE, CH), bf16),
                pltpu.VMEM((EXT, TILE, CH), bf16),
                pltpu.VMEM((2, 2, GT, TILE, CH), bf16),
                pltpu.VMEM((2 * GT * TILE, ATOMS), bf16),
                pltpu.VMEM((TILES, NB, TILE, NEI * TILE), bf16),
                pltpu.VMEM((TILES, TILE, NEI * TILE), f32),
                pltpu.VMEM((NEI * TILE, CH), bf16),
                pltpu.VMEM((TILE, NEI * TILE), f32),
                pltpu.VMEM((3, TILE, TILE), f32),
                pltpu.VMEM((TILES, TILE, CH), bf16),
                pltpu.VMEM((TILES, TILE, CH), bf16),
                pltpu.VMEM((8, ATOMS), f32),
                pltpu.VMEM((2, 8, ATOMS), f32),
                pltpu.VMEM((3, ATOMS), f32),
                pltpu.VMEM((2, 3, ATOMS), f32),
                pltpu.SemaphoreType.DMA((10,)),
                pltpu.SemaphoreType.DMA((10,)),
            ],
            compiler_params=pltpu.CompilerParams(
                collective_id=0, has_side_effects=True, vmem_limit_bytes=48 * 1024 * 1024
            ),
            name="md_step",
        )(*args)

    in_specs = (
        P("rep", None, "dom"),
        P("rep", None, "dom"),
        P("rep", None, "dom"),
        P("rep", "dom"),
        P("rep", "dom"),
        P("rep", "dom", None),
        P("rep", "dom"),
        P(), P(), P(), P(), P(), P(), P(), P(), P(), P(),
    )
    out_specs = (P("rep", None, "dom"), P("rep", None, "dom"), P("rep", None, "dom"))
    return jax.shard_map(local, mesh=mesh, in_specs=in_specs, out_specs=out_specs, check_vma=False)
```

time: 172 us -> 58.6 us (0.34)
  the two profiles are of different devices: /device:TPU:280 before, /device:TPU:1 now
where the time goes in v1:
time: 58.6 us; the launch traced here: 58.1 us
  Pallas kernels  51 us (87%)
  local copies, waits for them, and re-layouts  6.39 us (11%)
  between operations  0.8 us (1%)
    pallas_call x1, Pallas kernels, local(): pl.pallas_call(kernel, out_shape=(out, out, out), in_specs=[vmem, vmem, v...  51 us
    unnamed x30, local copies, waits for them, and re-layouts  4.55 us
    pallas_call x3, local copies, waits for them, and re-layouts, local(): pl.pallas_call(kernel, out_shape=(out, out, out), in_specs=[vmem, vmem, v...  1.84 us

profile of v1, /device:TPU:1, one launch (start us, length us, event | category | flops | bytes accessed | tf_op | source)
XLA Modules:
  0.0 58.1 jit_solution(15457167503226422994)
XLA Ops:
  0.6 0.0 copy-start
  0.6 0.8 %copy.23.refs_5_ = s32[1,8,4]{2,1,0:T(8,128)S(1)} copy(s32[1,8,4]{1,2,0:T(4,128)} %param.22) | data formatting | bytes 256 | tf_op args[5]
  1.4 0.7 %copy.20.refs_0_ = f32[1,3,1024]{2,1,0:T(4,128)S(1)} copy(f32[1,3,1024]{2,0,1:T(1,128)} %param.17) | data formatting | bytes 24576 | tf_op args[0]
  2.1 0.7 %copy.21.refs_1_ = f32[1,3,1024]{2,1,0:T(4,128)S(1)} copy(f32[1,3,1024]{2,0,1:T(1,128)} %param.18) | data formatting | bytes 24576 | tf_op args[1]
  2.9 0.0 copy-start.3
  2.9 0.0 copy-start.4
  2.9 0.0 copy-start.5
  2.9 0.0 copy-start.6
  2.9 0.0 copy-start.7
  2.9 0.0 copy-start.8
  2.9 0.0 copy-start.9
  2.9 0.0 copy-start.10
  2.9 0.0 copy-start.11
  2.9 0.0 copy-start.12
  3.0 0.8 %copy.22.refs_2_ = f32[1,3,1024]{2,1,0:T(4,128)S(1)} copy(f32[1,3,1024]{2,0,1:T(1,128)} %param.19) | data formatting | bytes 24576 | tf_op args[2]
  3.7 0.0 copy-done
  3.7 0.0 copy-done.3
  3.7 0.0 copy-done.4
  3.7 0.0 copy-done.5
  3.7 0.0 copy-done.6
  3.8 0.0 copy-done.7
  3.8 0.0 copy-done.8
  3.8 0.0 copy-done.9
  3.8 0.0 copy-done.10
  3.8 0.0 copy-done.11
  3.8 0.0 copy-done.12
  3.8 0.0 copy-start.1
  3.8 0.7 %copy-done.1 = bf16[128,128]{1,0:T(8,128)(2,1)S(1)} copy-done((bf16[128,128]{1,0:T(8,128)(2,1)S(1)}, bf16[128,128]{1,0:T(8,128)(2,1)}, u32[]{:S(2)}) %copy-start.1) | copy-done | bytes 32792
  4.6 0.0 copy-start.2
  4.6 0.8 %copy-done.2 = bf16[128,128]{1,0:T(8,128)(2,1)S(1)} copy-done((bf16[128,128]{1,0:T(8,128)(2,1)S(1)}, bf16[128,128]{1,0:T(8,128)(2,1)}, u32[]{:S(2)}) %copy-start.2) | copy-done | bytes 32792
  5.3 51.0 %md_step.1 = (f32[1,3,1024]{2,1,0:T(4,128)S(1)}, f32[1,3,1024]{2,1,0:T(4,128)S(1)}, f32[1,3,1024]{2,1,0:T(4,128)S(1)}) custom-call(f32[1,3,1024]{2,1,0:T(4,128)S(1)} %copy.20.refs_0_, f32[1,3,1024]{2,1,0:T(4,128)S(1)} %copy.21.refs_1_, f32[1,3,1024]{2,1,0:T(4,128)S(1)} %copy.22.refs_2_, s32[1,1024]{1,0:T(1,128)S(1)} %copy-done.4, s32[1,768]{1,0:T(1,128)S(1)} %copy-done.6, ...), custom_call_target="tpu_custom_call" | custom-call | tf_op jit(solution)/shard_map/md_step/pallas_call | solution.py:341
  56.3 0.6 %copy.24 = f32[1,3,1024]{2,0,1:T(1,128)} copy(f32[1,3,1024]{2,1,0:T(4,128)S(1)} %get-tuple-element.3) | data formatting | bytes 24576 | tf_op jit(solution)/shard_map/md_step/pallas_call | solution.py:341
  56.9 0.6 %copy.25 = f32[1,3,1024]{2,0,1:T(1,128)} copy(f32[1,3,1024]{2,1,0:T(4,128)S(1)} %get-tuple-element.4) | data formatting | bytes 24576 | tf_op jit(solution)/shard_map/md_step/pallas_call | solution.py:341
  57.5 0.6 %copy.26 = f32[1,3,1024]{2,0,1:T(1,128)} copy(f32[1,3,1024]{2,1,0:T(4,128)S(1)} %get-tuple-element.5) | data formatting | bytes 24576 | tf_op jit(solution)/shard_map/md_step/pallas_call | solution.py:341
Async XLA Ops:
  0.6 3.1 %copy-start = (bf16[2,128,128]{2,1,0:T(8,128)(2,1)S(1)}, bf16[2,128,128]{2,1,0:T(8,128)(2,1)}, u32[]{:S(2)}) copy-start(bf16[2,128,128]{2,1,0:T(8,128)(2,1)} %refs_11_.1) | copy-start | bytes 196612
  2.9 0.9 %copy-start.3 = (f32[2,8,128]{2,1,0:T(8,128)S(1)}, f32[2,8,128]{2,1,0:T(8,128)}, u32[]{:S(2)}) copy-start(f32[2,8,128]{2,1,0:T(8,128)} %refs_9_.1) | copy-start | bytes 24580
  2.9 0.9 %copy-start.4 = (s32[1,1024]{1,0:T(1,128)S(1)}, s32[1,1024]{1,0:T(1,128)}, u32[]{:S(2)}) copy-start(s32[1,1024]{1,0:T(1,128)} %refs_3_.1) | copy-start | bytes 12292
  2.9 0.9 %copy-start.5 = (bf16[16,128]{1,0:T(8,128)(2,1)S(1)}, bf16[16,128]{1,0:T(8,128)(2,1)}, u32[]{:S(2)}) copy-start(bf16[16,128]{1,0:T(8,128)(2,1)} %refs_7_.1) | copy-start | bytes 12292
  2.9 0.9 %copy-start.6 = (s32[1,768]{1,0:T(1,128)S(1)}, s32[1,768]{1,0:T(1,128)}, u32[]{:S(2)}) copy-start(s32[1,768]{1,0:T(1,128)} %refs_4_.1) | copy-start | bytes 9220
  2.9 0.9 %copy-start.7 = (f32[2,128]{1,0:T(2,128)S(1)}, f32[2,128]{1,0:T(2,128)}, u32[]{:S(2)}) copy-start(f32[2,128]{1,0:T(2,128)} %refs_10_.1) | copy-start | bytes 3076
  2.9 0.9 %copy-start.8 = (s32[1,8]{1,0:T(1,128)S(1)}, s32[1,8]{1,0:T(1,128)}, u32[]{:S(2)}) copy-start(s32[1,8]{1,0:T(1,128)} %refs_6_.1) | copy-start | bytes 100
  2.9 0.9 %copy-start.9 = (f32[16]{0:T(128)S(1)}, f32[16]{0:T(128)}, u32[]{:S(2)}) copy-start(f32[16]{0:T(128)} %refs_8_.1) | copy-start | bytes 196
  2.9 0.9 %copy-start.10 = (f32[8]{0:T(128)S(1)}, f32[8]{0:T(128)}, u32[]{:S(2)}) copy-start(f32[8]{0:T(128)} %refs_14_.1) | copy-start | bytes 100
  2.9 0.9 %copy-start.11 = (f32[64]{0:T(128)S(1)}, f32[64]{0:T(128)}, u32[]{:S(2)}) copy-start(f32[64]{0:T(128)} %refs_15_.1) | copy-start | bytes 772
  2.9 0.9 %copy-start.12 = (s32[64]{0:T(128)S(1)}, s32[64]{0:T(128)}, u32[]{:S(2)}) copy-start(s32[64]{0:T(128)} %refs_16_.1) | copy-start | bytes 772
  3.8 0.8 %copy-start.1 = (bf16[128,128]{1,0:T(8,128)(2,1)S(1)}, bf16[128,128]{1,0:T(8,128)(2,1)}, u32[]{:S(2)}) copy-start(bf16[128,128]{1,0:T(8,128)(2,1)} %refs_12_.1) | copy-start | bytes 98308
  4.6 0.8 %copy-start.2 = (bf16[128,128]{1,0:T(8,128)(2,1)S(1)}, bf16[128,128]{1,0:T(8,128)(2,1)}, u32[]{:S(2)}) copy-start(bf16[128,128]{1,0:T(8,128)(2,1)} %refs_13_.1) | copy-start | bytes 98308

commit v2 on v1

v2 whole, which is shorter than its diff:
```python
import math

import jax
import jax.numpy as jnp
from jax import lax
from jax.experimental import pallas as pl
from jax.experimental.pallas import tpu as pltpu
from jax.sharding import PartitionSpec as P

NB = 8
TILE = 128
NEI = 4
TILES = 8
GT = 3
EXT = TILES + 2 * GT
ATOMS = TILES * TILE
SPECIES = 16
CH = 128
CHUNK = 32

slab_width = 1.5
time_step = 0.5
basis_width = 0.3
norm_eps = 1e-06
factor = 1.0 / math.sqrt(CH * NEI * TILE)

ROOT = math.sqrt(math.log2(math.e))
SCALE = ROOT / basis_width
TOP = (NB - 1) * ROOT
FAR = 1.0e3

MESH = pl.DeviceIdType.MESH


def columns(row):
    return jnp.broadcast_to(row, (TILE, TILE)).T


def pick(offset, own, low, high):
    return jnp.where(offset == 1, high, jnp.where(offset == -1, low, own))


def step_kernel(reps, doms, *refs):
    ins, refs = refs[:17], refs[17:]
    (pos_out, vel_out, frc_out), refs = refs[:3], refs[3:]
    held, refs = refs[:17], refs[17:]
    (
        loc_ref, spd_ref, frc_ref, kind_ref, ghost_ref, adj_ref, live_ref, vec_ref, inertia_ref,
        radial_ref, gain_ref, mix_ref, target_ref, source_ref, taper_ref, heat_ref, swap_ref,
    ) = held
    (
        posext, psend, xcol, hext, mid, keys, hsend, onehot, even, odd, env, hcat, msgs,
        scores, facc, last, query, state, state_in, fown, f_in, in_sem, send_sem, recv_sem,
    ) = refs
    rep = lax.axis_index("rep")
    dom = lax.axis_index("dom")
    rep_to = (rep + 1, rep - 1)
    has = (rep < reps - 1, rep > 0)
    dom_to = (lax.rem(dom + 1, doms), lax.rem(dom + doms - 1, doms))

    barrier = pltpu.get_barrier_semaphore()
    for side in range(2):
        pl.semaphore_signal(barrier, inc=1, device_id={"dom": dom_to[side]}, device_id_type=MESH)

        @pl.when(has[side])
        def _():
            pl.semaphore_signal(
                barrier, inc=1, device_id={"rep": rep_to[side]}, device_id_type=MESH
            )

    loads = [
        pltpu.make_async_copy(ins[i], held[i], in_sem.at[i]) for i in range(17)
    ]
    for c in loads:
        c.start()

    def copy(stage, side, axis, src, dst):
        to = dom_to[side] if axis == "dom" else rep_to[side]
        return pltpu.make_async_remote_copy(
            src_ref=src,
            dst_ref=dst,
            send_sem=send_sem.at[2 * stage + side],
            recv_sem=recv_sem.at[2 * stage + side],
            device_id={axis: to},
            device_id_type=MESH,
        )

    def ladder_start(copies):
        for side in range(2):
            pl.when(has[side])(copies[side].start)

    def ladder_wait(copies):
        for side in range(2):
            pl.when(has[side])(copies[side].wait_send)
            pl.when(has[1 - side])(copies[side].wait_recv)

    for i in (8, 3, 0, 1, 2):
        loads[i].wait()
    kinds = kind_ref[...]
    mass = jnp.zeros((1, ATOMS), jnp.float32)
    for s in range(SPECIES):
        mass = jnp.where(kinds == s, inertia_ref[s], mass)
    inv_mass = 1.0 / mass
    moved, half = [], []
    for axis in range(3):
        loc, spd, frc = loc_ref[axis], spd_ref[axis], frc_ref[axis]
        moved.append(loc + time_step * spd + 0.5 * time_step * time_step * frc * inv_mass)
        half.append(spd + 0.5 * time_step * frc * inv_mass)
    kindf = kinds.astype(jnp.float32)
    for t in range(TILES):
        lanes = slice(t * TILE, (t + 1) * TILE)
        posext[t] = jnp.zeros((8, TILE), jnp.float32)
        for axis in range(3):
            posext[t, axis : axis + 1, :] = moved[axis][:, lanes]
        posext[t, 3:4, :] = kindf[:, lanes]

    loads[4].wait()
    first_row = lax.broadcasted_iota(jnp.int32, (8, TILE), 0) == 0
    for side in range(2):
        for g in range(GT):
            start = ((1 - side) * GT + g) * TILE
            label = jnp.broadcast_to(ghost_ref[:, start : start + TILE], (8, TILE))
            place = label & (TILE - 1)
            owner = label >> 7
            out = jnp.zeros((8, TILE), jnp.float32)
            for t in range(TILES):
                got = jnp.take_along_axis(posext[t], place, axis=1, mode="promise_in_bounds")
                out = jnp.where(owner == t, got, out)
            shift = slab_width if side == 1 else -slab_width
            psend[side, g] = jnp.where(first_row, out + shift, out)

    pl.semaphore_wait(barrier, 2 + has[0].astype(jnp.int32) + has[1].astype(jnp.int32))
    pos_copies = [
        copy(0, side, "dom", psend.at[side], posext.at[pl.ds(TILES + GT * side, GT)])
        for side in range(2)
    ]
    for c in pos_copies:
        c.start()

    for axis in range(3):
        state[axis] = moved[axis]
        state[3 + axis] = half[axis]
    state[6] = inv_mass
    state_copies = [copy(1, side, "rep", state, state_in.at[side]) for side in range(2)]
    ladder_start(state_copies)
    for side in range(2):

        @pl.when(jnp.logical_not(has[1 - side]))
        def _():
            state_in[side] = jnp.zeros((7, 1, ATOMS), jnp.float32)
            f_in[side] = jnp.zeros((3, 1, ATOMS), jnp.float32)

    lane = lax.broadcasted_iota(jnp.int32, (TILE, TILE), 1)
    lanef = lane.astype(jnp.float32)
    loads[7].wait()
    vectors = jnp.concatenate([vec_ref[...], jnp.zeros((TILE - SPECIES, CH), jnp.bfloat16)], axis=0)

    def embed(s):
        hot = jnp.where(columns(posext[s, 3:4, :]) == lanef, 1.0, 0.0).astype(jnp.bfloat16)
        hext[s] = jnp.dot(hot, vectors, preferred_element_type=jnp.float32).astype(jnp.bfloat16)

    def own_tile(t, _):
        for axis in range(3):
            xcol[t, axis] = columns(posext[t, axis : axis + 1, :])
        embed(t)
        return 0

    lax.fori_loop(0, TILES, own_tile, 0)

    for g in range(2 * GT):
        labels = columns(ghost_ref[:, g * TILE : (g + 1) * TILE])
        for t in range(TILES):
            hot = jnp.where(labels == lane + t * TILE, 1.0, 0.0).astype(jnp.bfloat16)
            onehot[t, g * TILE : (g + 1) * TILE, :] = hot

    for i in (5, 6, 9, 10, 11, 12, 13, 14, 15, 16):
        loads[i].wait()
    for c in pos_copies:
        c.wait()

    def fill_basis(t, buffer, slot):
        for k in range(NEI):
            far = posext[adj_ref[0, k, t]]
            dead = jnp.clip(k + 1 - live_ref[0, t], 0, 1).astype(jnp.float32) * FAR
            xj, yj, zj = far[0:1, :] + dead, far[1:2, :], far[2:3, :]
            for c in range(TILE // CHUNK):
                rows = slice(c * CHUNK, (c + 1) * CHUNK)
                dx = xj - xcol[t, 0, rows, :]
                dy = yj - xcol[t, 1, rows, :]
                dz = zj - xcol[t, 2, rows, :]
                square = dx * dx + dy * dy + dz * dz
                a = square * lax.rsqrt(jnp.maximum(square, 1e-30)) * SCALE
                top = a - TOP
                g = jnp.exp2(top * (TOP - a))
                q = jnp.exp2(a * (-2.0 * ROOT))
                for b in range(NB - 1, -1, -1):
                    buffer[slot, k, b, rows, :] = g.astype(jnp.bfloat16)
                    if b:
                        g = g * (q * math.exp(2 * b - 1))

    def sum_messages(layer, t, buffer, slot, source, parity):
        for k in range(NEI):
            hcat[parity, k * TILE : (k + 1) * TILE, :] = source[adj_ref[0, k, t]]
        flat = jnp.concatenate(
            [buffer[slot, k].reshape(NB * TILE, TILE) for k in range(NEI)], axis=1
        )
        summed = jnp.dot(flat, hcat[parity], preferred_element_type=jnp.float32)
        radial = radial_ref[layer]
        messages = radial[0:1, :] * summed[0:TILE, :]
        for b in range(1, NB):
            messages = messages + radial[b : b + 1, :] * summed[b * TILE : (b + 1) * TILE, :]
        msgs[parity] = messages

    def refresh(layer, t, source, parity):
        messages = msgs[parity]
        inverse = lax.rsqrt(jnp.mean(messages * messages, axis=-1, keepdims=True) + norm_eps)
        scaled = messages * inverse * gain_ref[layer : layer + 1, :]
        activation = (scaled / (1.0 + jnp.exp(-scaled))).astype(jnp.bfloat16)
        return (
            source[t].astype(jnp.float32)
            + jnp.dot(activation, mix_ref[layer], preferred_element_type=jnp.float32)
        ).astype(jnp.bfloat16)

    halves = (even, odd)

    def fill(t, u, parity):
        fill_basis(t, halves[parity], u)

    def run_layer(layer, source, finish, prepare):
        def gather(t, u, parity):
            sum_messages(layer, t, halves[parity], u, source, parity)

        def end(t, parity):
            finish(t, refresh(layer, t, source, parity))

        if prepare:
            fill(1, 0, 1)
        gather(0, 0, 0)

        def pair(u, _):
            if prepare:
                fill(2 * u + 2, u + 1, 0)
            gather(2 * u + 1, u, 1)
            end(2 * u, 0)
            if prepare:
                fill(2 * u + 3, u + 1, 1)
            gather(2 * u + 2, u + 1, 0)
            end(2 * u + 1, 1)
            return 0

        lax.fori_loop(0, TILES // 2 - 1, pair, 0)
        gather(TILES - 1, TILES // 2 - 1, 1)
        end(TILES - 2, 0)
        end(TILES - 1, 1)

    fill(0, 0, 0)
    for s in range(TILES, EXT):
        embed(s)

    def keep_mid(t, hidden):
        mid[t] = hidden

    run_layer(0, hext, keep_mid, True)

    def export(stage, rows, buffer, slot):
        copies = []
        for side in range(2):
            start = (1 - side) * GT * TILE
            hot = jnp.concatenate(
                [onehot[t, start : start + GT * TILE, :] for t in range(TILES)], axis=1
            )
            packed = jnp.dot(hot, rows, preferred_element_type=jnp.float32)
            hsend[slot, side] = packed.astype(jnp.bfloat16).reshape(GT, TILE, CH)
            c = copy(
                stage, side, "dom", hsend.at[slot, side], buffer.at[pl.ds(TILES + GT * side, GT)]
            )
            c.start()
            copies.append(c)
        return copies

    mid_copies = export(2, mid[0:TILES].reshape(ATOMS, CH), mid, 0)

    def fill_env(u, _):
        for parity in range(2):
            for k in range(NEI):
                total = taper_ref[0] * halves[parity][u, k, 0].astype(jnp.float32)
                for b in range(1, NB):
                    total = total + taper_ref[b] * halves[parity][u, k, b].astype(jnp.float32)
                env[2 * u + parity, k] = total * factor
        return 0

    lax.fori_loop(0, TILES // 2, fill_env, 0)

    for c in mid_copies:
        c.wait()

    def keep_last(t, hidden):
        last[t] = hidden
        keys[t] = jnp.dot(
            hidden, source_ref[...], preferred_element_type=jnp.float32
        ).astype(jnp.bfloat16)

    run_layer(1, mid, keep_last, False)
    key_copies = export(3, keys[0:TILES].reshape(ATOMS, CH), keys, 1)

    query[...] = (
        jnp.dot(
            last[...].reshape(ATOMS, CH), target_ref[...], preferred_element_type=jnp.float32
        )
        .astype(jnp.bfloat16)
        .reshape(TILES, TILE, CH)
    )
    ladder_wait(state_copies)
    partner = swap_ref[rep]
    offset = jnp.full((1, ATOMS), partner - rep, jnp.int32)
    for axis in range(3):
        pos_out[axis] = pick(offset, state[axis], state_in[0, axis], state_in[1, axis])
    quotient = jnp.sqrt(
        jnp.full((1, ATOMS), heat_ref[rep], jnp.float32)
        / jnp.full((1, ATOMS), heat_ref[partner], jnp.float32)
    )

    for c in key_copies:
        c.wait()

    def force_pair(u, _):
        for parity in range(2):
            t = 2 * u + parity
            for k in range(NEI):
                hcat[parity, k * TILE : (k + 1) * TILE, :] = keys[adj_ref[0, k, t]]
            scores[parity] = lax.dot_general(
                query[t],
                hcat[parity],
                (((1,), (1,)), ((), ())),
                preferred_element_type=jnp.float32,
            )
            fars = [posext[adj_ref[0, k, t]] for k in range(NEI)]
            for c in range(TILE // CHUNK):
                rows = slice(c * CHUNK, (c + 1) * CHUNK)
                weights = [
                    scores[parity, rows, k * TILE : (k + 1) * TILE] * env[t, k, rows, :]
                    for k in range(NEI)
                ]
                for axis in range(3):
                    near = xcol[t, axis, rows, :]
                    total = weights[0] * (fars[0][axis : axis + 1, :] - near)
                    for k in range(1, NEI):
                        total = total + weights[k] * (fars[k][axis : axis + 1, :] - near)
                    facc[parity, axis, rows, :] = total
            for axis in range(3):
                fown[axis, :, pl.ds(pl.multiple_of(t * TILE, TILE), TILE)] = jnp.sum(
                    facc[parity, axis].T, axis=0, keepdims=True
                )
        return 0

    lax.fori_loop(0, TILES // 2, force_pair, 0)

    f_copies = [copy(4, side, "rep", fown, f_in.at[side]) for side in range(2)]
    ladder_start(f_copies)
    ladder_wait(f_copies)
    inv_of = pick(offset, state[6], state_in[0, 6], state_in[1, 6])
    for axis in range(3):
        force = pick(offset, fown[axis], f_in[0, axis], f_in[1, axis])
        half_of = pick(offset, state[3 + axis], state_in[0, 3 + axis], state_in[1, 3 + axis])
        frc_out[axis] = force
        vel_out[axis] = (half_of + 0.5 * time_step * force * inv_of) * quotient


def solution(mesh):
    reps, doms = mesh.shape["rep"], mesh.shape["dom"]

    def kernel(*refs):
        step_kernel(reps, doms, *refs)

    def local(*args):
        args = list(args)
        for i in range(3):
            args[i] = jnp.transpose(args[i], (1, 0, 2))
        args[5] = jnp.transpose(args[5], (0, 2, 1))
        vmem = pl.BlockSpec(memory_space=pltpu.VMEM)
        hbm = pl.BlockSpec(memory_space=pltpu.HBM)
        out = jax.ShapeDtypeStruct((3, 1, ATOMS), jnp.float32)
        f32, bf16 = jnp.float32, jnp.bfloat16
        scalar = (5, 6, 8, 14, 15, 16)
        held = [
            (pltpu.SMEM if i in scalar else pltpu.VMEM)(x.shape, x.dtype)
            for i, x in enumerate(args)
        ]
        outs = pl.pallas_call(
            kernel,
            out_shape=(out, out, out),
            in_specs=[hbm] * 17,
            out_specs=(vmem, vmem, vmem),
            scratch_shapes=held
            + [
                pltpu.VMEM((EXT, 8, TILE), f32),
                pltpu.VMEM((2, GT, 8, TILE), f32),
                pltpu.VMEM((TILES, 3, TILE, TILE), f32),
                pltpu.VMEM((EXT, TILE, CH), bf16),
                pltpu.VMEM((EXT, TILE, CH), bf16),
                pltpu.VMEM((EXT, TILE, CH), bf16),
                pltpu.VMEM((2, 2, GT, TILE, CH), bf16),
                pltpu.VMEM((TILES, 2 * GT * TILE, TILE), bf16),
                pltpu.VMEM((TILES // 2, NEI, NB, TILE, TILE), bf16),
                pltpu.VMEM((TILES // 2, NEI, NB, TILE, TILE), bf16),
                pltpu.VMEM((TILES, NEI, TILE, TILE), f32),
                pltpu.VMEM((2, NEI * TILE, CH), bf16),
                pltpu.VMEM((2, TILE, CH), f32),
                pltpu.VMEM((2, TILE, NEI * TILE), f32),
                pltpu.VMEM((2, 3, TILE, TILE), f32),
                pltpu.VMEM((TILES, TILE, CH), bf16),
                pltpu.VMEM((TILES, TILE, CH), bf16),
                pltpu.VMEM((7, 1, ATOMS), f32),
                pltpu.VMEM((2, 7, 1, ATOMS), f32),
                pltpu.VMEM((3, 1, ATOMS), f32),
                pltpu.VMEM((2, 3, 1, ATOMS), f32),
                pltpu.SemaphoreType.DMA((17,)),
                pltpu.SemaphoreType.DMA((10,)),
                pltpu.SemaphoreType.DMA((10,)),
            ],
            compiler_params=pltpu.CompilerParams(
                collective_id=0, has_side_effects=True, vmem_limit_bytes=67043328
            ),
            name="md_step",
        )(*args)
        return tuple(jnp.transpose(x, (1, 0, 2)) for x in outs)

    in_specs = (
        P("rep", None, "dom"),
        P("rep", None, "dom"),
        P("rep", None, "dom"),
        P("rep", "dom"),
        P("rep", "dom"),
        P("rep", "dom", None),
        P("rep", "dom"),
        P(), P(), P(), P(), P(), P(), P(), P(), P(), P(),
    )
    out_specs = (P("rep", None, "dom"), P("rep", None, "dom"), P("rep", None, "dom"))
    return jax.shard_map(local, mesh=mesh, in_specs=in_specs, out_specs=out_specs, check_vma=False)
```

time: 58.6 us -> 44.8 us (0.76)
  Pallas kernels: 51 us -> 41.2 us
  local copies, waits for them, and re-layouts: 6.39 us -> 2.63 us
    pallas_call x1, Pallas kernels: 51 us -> 41.2 us  [local(): pl.pallas_call(kernel, out_shape=(out, out, out), in_specs=[hbm] * 17, ou...]
    unnamed x30 -> x7, local copies, waits for them, and re-layouts: 4.55 us -> 2.63 us
    pallas_call x3 -> x0, local copies, waits for them, and re-layouts: 1.84 us -> none  [local(): pl.pallas_call(kernel, out_shape=(out, out, out), in_specs=[vmem, vmem, v...]
where the time goes in v2:
time: 44.8 us; the launch traced here: 44.5 us
  Pallas kernels  41.2 us (92%)
  local copies, waits for them, and re-layouts  2.63 us (6%)
  between operations  0.66 us (1%)
    pallas_call x1, Pallas kernels, local(): pl.pallas_call(kernel, out_shape=(out, out, out), in_specs=[hbm] * 17, ou...  41.2 us
    unnamed x7, local copies, waits for them, and re-layouts  2.63 us

profile of v2, /device:TPU:1, one launch (start us, length us, event | category | flops | bytes accessed | tf_op | source)
XLA Modules:
  0.0 44.5 jit_solution(10453854985867600117)
XLA Ops:
  0.6 41.2 %md_step.1 = (f32[3,1,1024]{2,1,0:T(1,128)}, f32[3,1,1024]{2,1,0:T(1,128)}, f32[3,1,1024]{2,1,0:T(1,128)}) custom-call(f32[3,1,1024]{2,1,0:T(1,128)} %bitcast.7, f32[3,1,1024]{2,1,0:T(1,128)} %bitcast.8, f32[3,1,1024]{2,1,0:T(1,128)} %bitcast.9, s32[1,1024]{1,0:T(1,128)} %refs_3_.1, s32[1,768]{1,0:T(1,128)} %refs_4_.1, s32[1,4,8]{2,1,0:T(4,128)} %bitcast.13, ...), custom_call_target="tpu_custom_call" | custom-call | tf_op jit(solution)/shard_map/md_step/pallas_call | solution.py:389
  41.9 0.0 copy-start.1
  41.9 1.3 %copy.23 = f32[1,3,1024]{2,0,1:T(1,128)} copy(f32[1,3,1024]{2,0,1:T(1,128)} %bitcast.12) | data formatting | bytes 24576
  43.2 0.0 copy-done.1
  43.2 0.0 copy-start
  43.2 0.6 %copy.24 = f32[1,3,1024]{2,0,1:T(1,128)} copy(f32[1,3,1024]{2,0,1:T(1,128)S(1)} %bitcast.11) | data formatting | bytes 24576
  43.8 0.1 copy-done
  43.9 0.6 %copy.25 = f32[1,3,1024]{2,0,1:T(1,128)} copy(f32[1,3,1024]{2,0,1:T(1,128)S(1)} %bitcast.10) | data formatting | bytes 24576
Async XLA Ops:
  41.9 1.3 %copy-start.1 = (f32[3,1,1024]{2,1,0:T(1,128)S(1)}, f32[3,1,1024]{2,1,0:T(1,128)}, u32[]{:S(2)}) copy-start(f32[3,1,1024]{2,1,0:T(1,128)} %get-tuple-element.7) | copy-start | bytes 36868
  43.2 0.7 %copy-start = (f32[3,1,1024]{2,1,0:T(1,128)S(1)}, f32[3,1,1024]{2,1,0:T(1,128)}, u32[]{:S(2)}) copy-start(f32[3,1,1024]{2,1,0:T(1,128)} %get-tuple-element.8) | copy-start | bytes 36868

commit v3 on v2

v3 whole, which is shorter than its diff:
```python
import math

import jax
import jax.numpy as jnp
from jax import lax
from jax.experimental import pallas as pl
from jax.experimental.pallas import tpu as pltpu
from jax.sharding import PartitionSpec as P

NB = 8
TILE = 128
NEI = 4
TILES = 8
GT = 3
EXT = TILES + 2 * GT
ATOMS = TILES * TILE
SPECIES = 16
CH = 128
CHUNK = 32

slab_width = 1.5
time_step = 0.5
basis_width = 0.3
norm_eps = 1e-06
factor = 1.0 / math.sqrt(CH * NEI * TILE)

ROOT = math.sqrt(math.log2(math.e))
SCALE = ROOT / basis_width
TOP = (NB - 1) * ROOT
FAR = 1.0e3
UNFOLD = [math.exp((NB - 1) ** 2 - b * b) for b in range(NB)]

MESH = pl.DeviceIdType.MESH


def columns(row):
    return jnp.broadcast_to(row, (TILE, TILE)).T


def pick(offset, own, low, high):
    return jnp.where(offset == 1, high, jnp.where(offset == -1, low, own))


def step_kernel(reps, doms, *refs):
    ins, refs = refs[:17], refs[17:]
    (result,), refs = refs[:1], refs[1:]
    held, refs = refs[:17], refs[17:]
    (
        loc_ref, spd_ref, frc_ref, kind_ref, ghost_ref, adj_ref, live_ref, vec_ref, inertia_ref,
        radial_ref, gain_ref, mix_ref, target_ref, source_ref, taper_ref, heat_ref, swap_ref,
    ) = held
    (
        posext, psend, xcol, hext, mid, keys, hsend, onehot, even, odd, lever, hcat, msgs,
        facc, last, query, state, late, state_in, late_in, pos_in, aux, aux_in, chosen, aux_smem,
        radial, in_sem, aux_sem, send_sem, recv_sem,
    ) = refs
    rep = lax.axis_index("rep")
    dom = lax.axis_index("dom")
    has = (rep < reps - 1, rep > 0)
    dom_to = (lax.rem(dom + 1, doms), lax.rem(dom + doms - 1, doms))
    ladder = ((0, None, None), (1, has[0], has[1]), (-1, has[1], has[0]))

    def when(condition, action):
        if condition is None:
            action()
        else:
            pl.when(condition)(action)

    barrier = pltpu.get_barrier_semaphore()

    def greet(step, side):
        to = {"rep": rep + step} if side is None else {"rep": rep + step, "dom": dom_to[side]}
        pl.semaphore_signal(barrier, inc=1, device_id=to, device_id_type=MESH)

    for step, there, _ in ladder:
        for side in (0, 1) if step == 0 else (0, 1, None):
            when(there, lambda step=step, side=side: greet(step, side))

    loads = [
        pltpu.make_async_copy(ins[i], held[i], in_sem.at[i]) for i in range(17)
    ]
    for c in loads:
        c.start()

    def copy(number, to, src, dst):
        return pltpu.make_async_remote_copy(
            src_ref=src,
            dst_ref=dst,
            send_sem=send_sem.at[number],
            recv_sem=recv_sem.at[number],
            device_id=to,
            device_id_type=MESH,
        )

    for i in (8, 3, 0, 1, 2):
        loads[i].wait()
    kinds = kind_ref[...]
    mass = jnp.zeros((1, ATOMS), jnp.float32)
    for s in range(SPECIES):
        mass = jnp.where(kinds == s, inertia_ref[s], mass)
    inv_mass = 1.0 / mass
    moved, half = [], []
    for axis in range(3):
        loc, spd, frc = loc_ref[axis], spd_ref[axis], frc_ref[axis]
        moved.append(loc + time_step * spd + 0.5 * time_step * time_step * frc * inv_mass)
        half.append(spd + 0.5 * time_step * frc * inv_mass)
    kindf = kinds.astype(jnp.float32)
    for t in range(TILES):
        lanes = slice(t * TILE, (t + 1) * TILE)
        posext[t] = jnp.zeros((8, TILE), jnp.float32)
        for axis in range(3):
            posext[t, axis : axis + 1, :] = moved[axis][:, lanes]
        posext[t, 3:4, :] = kindf[:, lanes]

    loads[4].wait()
    first_row = lax.broadcasted_iota(jnp.int32, (8, TILE), 0) == 0
    for side in range(2):
        for g in range(GT):
            start = ((1 - side) * GT + g) * TILE
            label = jnp.broadcast_to(ghost_ref[:, start : start + TILE], (8, TILE))
            place = label & (TILE - 1)
            owner = label >> 7
            out = jnp.zeros((8, TILE), jnp.float32)
            for t in range(TILES):
                got = jnp.take_along_axis(posext[t], place, axis=1, mode="promise_in_bounds")
                out = jnp.where(owner == t, got, out)
            shift = slab_width if side == 1 else -slab_width
            psend[side, g] = jnp.where(first_row, out + shift, out)

    for axis in range(3):
        state[axis] = moved[axis]
        late[axis] = half[axis]
    state[3] = kindf
    late[3] = inv_mass
    late[4, :, 0 : 2 * GT * TILE] = ghost_ref[...].astype(jnp.float32)
    late[4, :, 2 * GT * TILE :] = jnp.zeros((1, ATOMS - 2 * GT * TILE), jnp.float32)
    loads[5].wait()
    loads[6].wait()
    aux[...] = jnp.zeros((8, TILE), jnp.int32)
    aux[0:NEI, 0:TILES] = adj_ref[0]
    aux[NEI : NEI + 1, 0:TILES] = live_ref[...]

    pl.semaphore_wait(barrier, 2 + 3 * (has[0].astype(jnp.int32) + has[1].astype(jnp.int32)))
    copies = []
    for n, (step, there, comes) in enumerate(ladder):
        for side in range(2):
            to = {"rep": rep + step, "dom": dom_to[side]}
            copies.append((copy(2 * n + side, to, psend.at[side], pos_in.at[n, side]), there, comes))
    for n, (step, there, comes) in enumerate(ladder[1:]):
        to = {"rep": rep + step}
        copies.append((copy(6 + n, to, state, state_in.at[n]), there, comes))
        copies.append((copy(8 + n, to, aux, aux_in.at[n]), there, comes))
    late_copies = [
        (copy(14 + n, {"rep": rep + step}, late, late_in.at[n]), there, comes)
        for n, (step, there, comes) in enumerate(ladder[1:])
    ]
    for c, there, _ in copies + late_copies:
        when(there, c.start)
    for n in (1, 2):

        @pl.when(jnp.logical_not(ladder[n][2]))
        def _():
            pos_in[n] = jnp.zeros((2, GT, 8, TILE), jnp.float32)
            state_in[n - 1] = jnp.zeros((4, 1, ATOMS), jnp.float32)
            late_in[n - 1] = jnp.zeros((5, 1, ATOMS), jnp.float32)
            aux_in[n - 1] = jnp.zeros((8, TILE), jnp.int32)

    for i in (7, 9, 10, 11, 12, 13, 14, 15, 16):
        loads[i].wait()
    lanef = lax.broadcasted_iota(jnp.int32, (TILE, TILE), 1).astype(jnp.float32)
    row = lax.broadcasted_iota(jnp.int32, (NB, CH), 0)
    scales = jnp.zeros((NB, CH), jnp.float32)
    for b in range(NB):
        scales = jnp.where(row == b, UNFOLD[b], scales)
    vectors = jnp.concatenate([vec_ref[...], jnp.zeros((TILE - SPECIES, CH), jnp.bfloat16)], axis=0)
    partner = swap_ref[rep]
    quotient = jnp.sqrt(
        jnp.full((1, ATOMS), heat_ref[rep], jnp.float32)
        / jnp.full((1, ATOMS), heat_ref[partner], jnp.float32)
    )
    for c, there, comes in copies:
        when(there, c.wait_send)
        when(comes, c.wait_recv)

    offset = jnp.full((8, TILE), partner - rep, jnp.int32)
    aux[...] = pick(offset, aux[...], aux_in[0], aux_in[1])
    to_smem = pltpu.make_async_copy(aux, aux_smem, aux_sem)
    to_smem.start()
    for side in range(2):
        for g in range(GT):
            posext[TILES + GT * side + g] = pick(
                offset, pos_in[0, side, g], pos_in[1, side, g], pos_in[2, side, g]
            )
    offset = jnp.full((1, ATOMS), partner - rep, jnp.int32)
    for row in range(4):
        chosen[row] = pick(offset, state[row], state_in[0, row], state_in[1, row])
    for t in range(TILES):
        lanes = slice(t * TILE, (t + 1) * TILE)
        for axis in range(3):
            posext[t, axis : axis + 1, :] = chosen[axis, :, lanes]
        posext[t, 3:4, :] = chosen[3, :, lanes]
    for s in range(EXT):
        posext[s, 4:7, :] = posext[s, 0:3, :] * SCALE
    for layer in range(2):
        radial[layer] = radial_ref[layer] * scales
    for axis in range(3):
        result[axis] = chosen[axis]

    def take_late():
        for c, there, comes in late_copies:
            when(there, c.wait_send)
            when(comes, c.wait_recv)
        for row in range(5):
            chosen[4 + row] = pick(offset, late[row], late_in[0, row], late_in[1, row])

    def embed(s):
        hot = jnp.where(columns(posext[s, 3:4, :]) == lanef, 1.0, 0.0).astype(jnp.bfloat16)
        hext[s] = jnp.dot(hot, vectors, preferred_element_type=jnp.float32).astype(jnp.bfloat16)

    def fill_onehot():
        for g in range(2 * GT):
            labels = columns(chosen[8, :, g * TILE : (g + 1) * TILE])
            for t in range(TILES):
                hot = jnp.where(labels == lanef + float(t * TILE), 1.0, 0.0).astype(jnp.bfloat16)
                onehot[t, g * TILE : (g + 1) * TILE, :] = hot

    to_smem.wait()

    def fill_basis(t, buffer, slot):
        for axis in range(3):
            xcol[t, axis] = columns(posext[t, 4 + axis : 5 + axis, :])
        for k in range(NEI):
            far = posext[aux_smem[k, t]]
            dead = jnp.clip(k + 1 - aux_smem[NEI, t], 0, 1).astype(jnp.float32) * FAR
            xj, yj, zj = far[4:5, :] + dead, far[5:6, :], far[6:7, :]
            for c in range(TILE // CHUNK):
                rows = slice(c * CHUNK, (c + 1) * CHUNK)
                dx = xj - xcol[t, 0, rows, :]
                dy = yj - xcol[t, 1, rows, :]
                dz = zj - xcol[t, 2, rows, :]
                square = dx * dx + dy * dy + dz * dz
                a = square * lax.rsqrt(jnp.maximum(square, 1e-30))
                top = a - TOP
                g = jnp.exp2(top * (TOP - a))
                q = jnp.exp2(a * (-2.0 * ROOT))
                for b in range(NB - 1, -1, -1):
                    buffer[slot, k, b, rows, :] = g.astype(jnp.bfloat16)
                    if b:
                        g = g * q

    def sum_messages(layer, t, buffer, slot, source, parity):
        for k in range(NEI):
            hcat[parity, k * TILE : (k + 1) * TILE, :] = source[aux_smem[k, t]]
        parts = []
        for k in range(0, NEI, 2):
            flat = jnp.concatenate(
                [buffer[slot, k + i].reshape(NB * TILE, TILE) for i in range(2)], axis=1
            )
            parts.append(
                jnp.dot(
                    flat,
                    hcat[parity, k * TILE : (k + 2) * TILE, :],
                    preferred_element_type=jnp.float32,
                )
            )
        summed = parts[0] + parts[1]
        weights = radial[layer]
        messages = weights[0:1, :] * summed[0:TILE, :]
        for b in range(1, NB):
            messages = messages + weights[b : b + 1, :] * summed[b * TILE : (b + 1) * TILE, :]
        msgs[parity] = messages

    def refresh(layer, t, source, parity):
        messages = msgs[parity]
        inverse = lax.rsqrt(jnp.mean(messages * messages, axis=-1, keepdims=True) + norm_eps)
        scaled = messages * inverse * gain_ref[layer : layer + 1, :]
        activation = (scaled / (1.0 + jnp.exp(-scaled))).astype(jnp.bfloat16)
        return (
            source[t].astype(jnp.float32)
            + jnp.dot(activation, mix_ref[layer], preferred_element_type=jnp.float32)
        ).astype(jnp.bfloat16)

    halves = (even, odd)

    def fill(t, u, parity):
        fill_basis(t, halves[parity], u)

    def run_layer(layer, source, finish, prepare):
        def gather(t, u, parity):
            sum_messages(layer, t, halves[parity], u, source, parity)

        def end(t, parity):
            finish(t, refresh(layer, t, source, parity))

        if prepare:
            fill(1, 0, 1)
        gather(0, 0, 0)

        def pair(u, _):
            if prepare:
                fill(2 * u + 2, u + 1, 0)
            gather(2 * u + 1, u, 1)
            end(2 * u, 0)
            if prepare:
                fill(2 * u + 3, u + 1, 1)
            gather(2 * u + 2, u + 1, 0)
            end(2 * u + 1, 1)
            return 0

        lax.fori_loop(0, TILES // 2 - 1, pair, 0)
        if prepare:
            take_late()
            fill_onehot()
        gather(TILES - 1, TILES // 2 - 1, 1)
        end(TILES - 2, 0)
        end(TILES - 1, 1)

    fill(0, 0, 0)
    for s in range(EXT):
        embed(s)

    def keep_mid(t, hidden):
        mid[t] = hidden

    run_layer(0, hext, keep_mid, True)

    first = 1 - jnp.minimum(lax.rem(dom, doms // 2), 1)

    def export(stage, rows, buffer, slot):
        copies = []
        for turn in range(2):
            side = lax.rem(first + turn, 2)
            start = pl.multiple_of((1 - side) * GT * TILE, GT * TILE)
            hot = jnp.concatenate(
                [onehot[t, pl.ds(start, GT * TILE), :] for t in range(TILES)], axis=1
            )
            packed = jnp.dot(hot, rows, preferred_element_type=jnp.float32)
            hsend[slot, turn] = packed.astype(jnp.bfloat16).reshape(GT, TILE, CH)
            c = copy(
                2 * stage + side,
                {"dom": lax.rem(dom + 1 - 2 * side + doms, doms)},
                hsend.at[slot, turn],
                buffer.at[pl.ds(TILES + GT * side, GT)],
            )
            c.start()
            copies.append(c)
        return copies

    mid_copies = export(5, mid[0:TILES].reshape(ATOMS, CH), mid, 0)

    taper = [taper_ref[b] * (UNFOLD[b] * factor / SCALE) for b in range(NB)]

    def fill_lever(u, _):
        for parity in range(2):
            t = 2 * u + parity
            for k in range(NEI):
                far = posext[aux_smem[k, t]]
                for c in range(TILE // CHUNK):
                    rows = slice(c * CHUNK, (c + 1) * CHUNK)
                    total = taper[0] * halves[parity][u, k, 0, rows, :].astype(jnp.float32)
                    for b in range(1, NB):
                        total = total + taper[b] * halves[parity][u, k, b, rows, :].astype(
                            jnp.float32
                        )
                    for axis in range(3):
                        lever[t, k, axis, rows, :] = total * (
                            far[4 + axis : 5 + axis, :] - xcol[t, axis, rows, :]
                        )
        return 0

    lax.fori_loop(0, TILES // 2, fill_lever, 0)

    for c in mid_copies:
        c.wait()

    def keep_last(t, hidden):
        last[t] = hidden
        keys[t] = jnp.dot(
            hidden, source_ref[...], preferred_element_type=jnp.float32
        ).astype(jnp.bfloat16)

    run_layer(1, mid, keep_last, False)
    key_copies = export(6, keys[0:TILES].reshape(ATOMS, CH), keys, 1)

    query[...] = (
        jnp.dot(
            last[...].reshape(ATOMS, CH), target_ref[...], preferred_element_type=jnp.float32
        )
        .astype(jnp.bfloat16)
        .reshape(TILES, TILE, CH)
    )
    for c in key_copies:
        c.wait()

    def force_pair(u, _):
        for parity in range(2):
            t = 2 * u + parity
            for k in range(NEI):
                hcat[parity, k * TILE : (k + 1) * TILE, :] = keys[aux_smem[k, t]]
            scores = lax.dot_general(
                query[t],
                hcat[parity],
                (((1,), (1,)), ((), ())),
                preferred_element_type=jnp.float32,
            )
            for axis in range(3):
                total = scores[:, 0:TILE] * lever[t, 0, axis]
                for k in range(1, NEI):
                    total = total + scores[:, k * TILE : (k + 1) * TILE] * lever[t, k, axis]
                facc[parity, axis] = total
            lanes = pl.ds(pl.multiple_of(t * TILE, TILE), TILE)
            for axis in range(3):
                result[6 + axis, :, lanes] = jnp.sum(facc[parity, axis].T, axis=0, keepdims=True)
        return 0

    lax.fori_loop(0, TILES // 2, force_pair, 0)

    for axis in range(3):
        force = result[6 + axis]
        result[3 + axis] = (chosen[4 + axis] + 0.5 * time_step * force * chosen[7]) * quotient


def hand_out(packed, pos_out, vel_out, frc_out, sem):
    copies = [
        pltpu.make_async_copy(packed.at[pl.ds(3 * i, 3)], ref, sem.at[i])
        for i, ref in enumerate((pos_out, vel_out, frc_out))
    ]
    for c in copies:
        c.start()
    for c in copies:
        c.wait()


def solution(mesh):
    reps, doms = mesh.shape["rep"], mesh.shape["dom"]

    def kernel(*refs):
        step_kernel(reps, doms, *refs)

    def local(*args):
        args = list(args)
        for i in range(3):
            args[i] = jnp.transpose(args[i], (1, 0, 2))
        args[5] = jnp.transpose(args[5], (0, 2, 1))
        vmem = pl.BlockSpec(memory_space=pltpu.VMEM)
        hbm = pl.BlockSpec(memory_space=pltpu.HBM)
        out = jax.ShapeDtypeStruct((3, 1, ATOMS), jnp.float32)
        f32, bf16 = jnp.float32, jnp.bfloat16
        scalar = (8, 14, 15, 16)
        held = [
            (pltpu.SMEM if i in scalar else pltpu.VMEM)(x.shape, x.dtype)
            for i, x in enumerate(args)
        ]
        packed = pl.pallas_call(
            kernel,
            out_shape=jax.ShapeDtypeStruct((9, 1, ATOMS), jnp.float32),
            in_specs=[hbm] * 17,
            out_specs=vmem,
            scratch_shapes=held
            + [
                pltpu.VMEM((EXT, 8, TILE), f32),
                pltpu.VMEM((2, GT, 8, TILE), f32),
                pltpu.VMEM((TILES, 3, TILE, TILE), f32),
                pltpu.VMEM((EXT, TILE, CH), bf16),
                pltpu.VMEM((EXT, TILE, CH), bf16),
                pltpu.VMEM((EXT, TILE, CH), bf16),
                pltpu.VMEM((2, 2, GT, TILE, CH), bf16),
                pltpu.VMEM((TILES, 2 * GT * TILE, TILE), bf16),
                pltpu.VMEM((TILES // 2, NEI, NB, TILE, TILE), bf16),
                pltpu.VMEM((TILES // 2, NEI, NB, TILE, TILE), bf16),
                pltpu.VMEM((TILES, NEI, 3, TILE, TILE), f32),
                pltpu.VMEM((2, NEI * TILE, CH), bf16),
                pltpu.VMEM((2, TILE, CH), f32),
                pltpu.VMEM((2, 3, TILE, TILE), f32),
                pltpu.VMEM((TILES, TILE, CH), bf16),
                pltpu.VMEM((TILES, TILE, CH), bf16),
                pltpu.VMEM((4, 1, ATOMS), f32),
                pltpu.VMEM((5, 1, ATOMS), f32),
                pltpu.VMEM((2, 4, 1, ATOMS), f32),
                pltpu.VMEM((2, 5, 1, ATOMS), f32),
                pltpu.VMEM((3, 2, GT, 8, TILE), f32),
                pltpu.VMEM((8, TILE), jnp.int32),
                pltpu.VMEM((2, 8, TILE), jnp.int32),
                pltpu.VMEM((9, 1, ATOMS), f32),
                pltpu.SMEM((8, TILE), jnp.int32),
                pltpu.VMEM((2, NB, CH), f32),
                pltpu.SemaphoreType.DMA((17,)),
                pltpu.SemaphoreType.DMA,
                pltpu.SemaphoreType.DMA((16,)),
                pltpu.SemaphoreType.DMA((16,)),
            ],
            compiler_params=pltpu.CompilerParams(
                collective_id=0, has_side_effects=True, vmem_limit_bytes=66850000
            ),
            name="md_step",
        )(*args)
        outs = pl.pallas_call(
            hand_out,
            out_shape=(out, out, out),
            in_specs=[vmem],
            out_specs=(hbm, hbm, hbm),
            scratch_shapes=[pltpu.SemaphoreType.DMA((3,))],
            compiler_params=pltpu.CompilerParams(vmem_limit_bytes=1048576),
            name="hand_out",
        )(packed)
        return tuple(jnp.transpose(x, (1, 0, 2)) for x in outs)

    in_specs = (
        P("rep", None, "dom"),
        P("rep", None, "dom"),
        P("rep", None, "dom"),
        P("rep", "dom"),
        P("rep", "dom"),
        P("rep", "dom", None),
        P("rep", "dom"),
        P(), P(), P(), P(), P(), P(), P(), P(), P(), P(),
    )
    out_specs = (P("rep", None, "dom"), P("rep", None, "dom"), P("rep", None, "dom"))
    return jax.shard_map(local, mesh=mesh, in_specs=in_specs, out_specs=out_specs, check_vma=False)
```

time: 44.8 us -> 41.7 us (0.931)
  local copies, waits for them, and re-layouts: 2.63 us -> 0.76 us
  Pallas kernels: 41.2 us -> 40 us
    unnamed x7 -> x2, local copies, waits for them, and re-layouts: 2.63 us -> 0.76 us
    pallas_call x1 -> x2, Pallas kernels: 41.2 us -> 40 us  [the longest x1 39.4 us: local(): pl.pallas_call(kernel, out_shape=jax.ShapeDtypeStruct((9, 1, ATOMS), jnp....]
where the time goes in v3:
time: 41.7 us; the launch traced here: 41.4 us
  Pallas kernels  40 us (96%)
  local copies, waits for them, and re-layouts  0.76 us (2%)
  between operations  0.65 us (2%)
    pallas_call x1, Pallas kernels, local(): pl.pallas_call(kernel, out_shape=jax.ShapeDtypeStruct((9, 1, ATOMS), jnp....  39.4 us

profile of v3, /device:TPU:1, one launch (start us, length us, event | category | flops | bytes accessed | tf_op | source)
XLA Modules:
  0.0 41.4 jit_solution(6276129323294758074)
XLA Ops:
  0.6 39.4 %md_step.1.packed = f32[9,1,1024]{2,1,0:T(1,128)} custom-call(f32[3,1,1024]{2,1,0:T(1,128)} %bitcast.7, f32[3,1,1024]{2,1,0:T(1,128)} %bitcast.8, f32[3,1,1024]{2,1,0:T(1,128)} %bitcast.9, s32[1,1024]{1,0:T(1,128)} %refs_3_.1, s32[1,768]{1,0:T(1,128)} %refs_4_.1, s32[1,4,8]{2,1,0:T(4,128)} %bitcast.10, s32[1,8]{1,0:T(1,128)} %refs_6_.1, ...), custom_call_target="tpu_custom_call" | custom-call | tf_op jit(solution)/shard_map/md_step/pallas_call | solution.py:454
  40.0 0.0 copy-start
  40.1 0.8 %copy-done = f32[9,1,1024]{2,1,0:T(1,128)S(1)} copy-done((f32[9,1,1024]{2,1,0:T(1,128)S(1)}, f32[9,1,1024]{2,1,0:T(1,128)}, u32[]{:S(2)}) %copy-start) | copy-done | bytes 36888
  40.8 0.6 %hand_out.1 = (f32[3,1,1024]{2,1,0:T(1,128)}, f32[3,1,1024]{2,1,0:T(1,128)}, f32[3,1,1024]{2,1,0:T(1,128)}) custom-call(f32[9,1,1024]{2,1,0:T(1,128)S(1)} %copy-done), custom_call_target="tpu_custom_call" | custom-call | tf_op jit(solution)/shard_map/hand_out/pallas_call | solution.py:497
Async XLA Ops:
  40.0 0.8 %copy-start = (f32[9,1,1024]{2,1,0:T(1,128)S(1)}, f32[9,1,1024]{2,1,0:T(1,128)}, u32[]{:S(2)}) copy-start(f32[9,1,1024]{2,1,0:T(1,128)} %md_step.1.packed) | copy-start | bytes 110596

commit v4 on v3

--- a/solution.py
+++ b/solution.py
@@ -50,7 +50,7 @@
         radial_ref, gain_ref, mix_ref, target_ref, source_ref, taper_ref, heat_ref, swap_ref,
     ) = held
     (
-        posext, psend, xcol, hext, mid, keys, hsend, onehot, even, odd, lever, hcat, msgs,
+        posext, psend, xcol, hext, mid, hsend, onehot, even, odd, lever, hcat, msgs,
         facc, last, query, state, late, state_in, late_in, pos_in, aux, aux_in, chosen, aux_smem,
         radial, in_sem, aux_sem, send_sem, recv_sem,
     ) = refs
@@ -330,23 +330,25 @@
         copies = []
         for turn in range(2):
             side = lax.rem(first + turn, 2)
-            start = pl.multiple_of((1 - side) * GT * TILE, GT * TILE)
-            hot = jnp.concatenate(
-                [onehot[t, pl.ds(start, GT * TILE), :] for t in range(TILES)], axis=1
-            )
-            packed = jnp.dot(hot, rows, preferred_element_type=jnp.float32)
-            hsend[slot, turn] = packed.astype(jnp.bfloat16).reshape(GT, TILE, CH)
-            c = copy(
-                2 * stage + side,
-                {"dom": lax.rem(dom + 1 - 2 * side + doms, doms)},
-                hsend.at[slot, turn],
-                buffer.at[pl.ds(TILES + GT * side, GT)],
-            )
-            c.start()
-            copies.append(c)
+            to = {"dom": lax.rem(dom + 1 - 2 * side + doms, doms)}
+            for g in range(GT):
+                start = pl.multiple_of(((1 - side) * GT + g) * TILE, TILE)
+                hot = jnp.concatenate(
+                    [onehot[t, pl.ds(start, TILE), :] for t in range(TILES)], axis=1
+                )
+                packed = jnp.dot(hot, rows, preferred_element_type=jnp.float32)
+                hsend[slot, turn, g] = packed.astype(jnp.bfloat16)
+                c = copy(
+                    2 * GT * stage + GT * side + g,
+                    to,
+                    hsend.at[slot, turn, g],
+                    buffer.at[TILES + GT * side + g],
+                )
+                c.start()
+                copies.append(c)
         return copies
 
-    mid_copies = export(5, mid[0:TILES].reshape(ATOMS, CH), mid, 0)
+    mid_copies = export(3, mid[0:TILES].reshape(ATOMS, CH), mid, 0)
 
     taper = [taper_ref[b] * (UNFOLD[b] * factor / SCALE) for b in range(NB)]
 
@@ -375,20 +377,17 @@
 
     def keep_last(t, hidden):
         last[t] = hidden
-        keys[t] = jnp.dot(
-            hidden, source_ref[...], preferred_element_type=jnp.float32
-        ).astype(jnp.bfloat16)
 
     run_layer(1, mid, keep_last, False)
-    key_copies = export(6, keys[0:TILES].reshape(ATOMS, CH), keys, 1)
-
-    query[...] = (
-        jnp.dot(
-            last[...].reshape(ATOMS, CH), target_ref[...], preferred_element_type=jnp.float32
-        )
-        .astype(jnp.bfloat16)
-        .reshape(TILES, TILE, CH)
+    key_copies = export(4, last[0:TILES].reshape(ATOMS, CH), last, 1)
+
+    rows = last[0:TILES].reshape(ATOMS, CH)
+    asked = jnp.dot(rows, target_ref[...], preferred_element_type=jnp.float32).astype(jnp.bfloat16)
+    asked = lax.dot_general(
+        asked, source_ref[...], (((1,), (1,)), ((), ())), preferred_element_type=jnp.float32
     )
+    query[...] = asked.astype(jnp.bfloat16).reshape(TILES, TILE, CH)
+
     for c in key_copies:
         c.wait()
 
@@ -396,7 +395,7 @@
         for parity in range(2):
             t = 2 * u + parity
             for k in range(NEI):
-                hcat[parity, k * TILE : (k + 1) * TILE, :] = keys[aux_smem[k, t]]
+                hcat[parity, k * TILE : (k + 1) * TILE, :] = last[aux_smem[k, t]]
             scores = lax.dot_general(
                 query[t],
                 hcat[parity],
@@ -463,7 +462,6 @@
                 pltpu.VMEM((TILES, 3, TILE, TILE), f32),
                 pltpu.VMEM((EXT, TILE, CH), bf16),
                 pltpu.VMEM((EXT, TILE, CH), bf16),
-                pltpu.VMEM((EXT, TILE, CH), bf16),
                 pltpu.VMEM((2, 2, GT, TILE, CH), bf16),
                 pltpu.VMEM((TILES, 2 * GT * TILE, TILE), bf16),
                 pltpu.VMEM((TILES // 2, NEI, NB, TILE, TILE), bf16),
@@ -472,7 +470,7 @@
                 pltpu.VMEM((2, NEI * TILE, CH), bf16),
                 pltpu.VMEM((2, TILE, CH), f32),
                 pltpu.VMEM((2, 3, TILE, TILE), f32),
-                pltpu.VMEM((TILES, TILE, CH), bf16),
+                pltpu.VMEM((EXT, TILE, CH), bf16),
                 pltpu.VMEM((TILES, TILE, CH), bf16),
                 pltpu.VMEM((4, 1, ATOMS), f32),
                 pltpu.VMEM((5, 1, ATOMS), f32),
@@ -486,8 +484,8 @@
                 pltpu.VMEM((2, NB, CH), f32),
                 pltpu.SemaphoreType.DMA((17,)),
                 pltpu.SemaphoreType.DMA,
-                pltpu.SemaphoreType.DMA((16,)),
-                pltpu.SemaphoreType.DMA((16,)),
+                pltpu.SemaphoreType.DMA((30,)),
+                pltpu.SemaphoreType.DMA((30,)),
             ],
             compiler_params=pltpu.CompilerParams(
                 collective_id=0, has_side_effects=True, vmem_limit_bytes=66850000

time: 41.7 us -> 41 us (0.983)
  Pallas kernels: 40 us -> 39.3 us
    pallas_call x1, Pallas kernels: 39.4 us -> 38.7 us  [local(): pl.pallas_call(kernel, out_shape=jax.ShapeDtypeStruct((9, 1, ATOMS), jnp....]
where the time goes in v4:
time: 41 us; the launch traced here: 40.7 us
  Pallas kernels  39.3 us (96%)
  local copies, waits for them, and re-layouts  0.76 us (2%)
  between operations  0.65 us (2%)
    pallas_call x1, Pallas kernels, local(): pl.pallas_call(kernel, out_shape=jax.ShapeDtypeStruct((9, 1, ATOMS), jnp....  38.7 us

profile of v4, /device:TPU:1, one launch (start us, length us, event | category | flops | bytes accessed | tf_op | source)
XLA Modules:
  0.0 40.7 jit_solution(9106047859621017214)
XLA Ops:
  0.6 38.7 %md_step.1.packed = f32[9,1,1024]{2,1,0:T(1,128)} custom-call(f32[3,1,1024]{2,1,0:T(1,128)} %bitcast.7, f32[3,1,1024]{2,1,0:T(1,128)} %bitcast.8, f32[3,1,1024]{2,1,0:T(1,128)} %bitcast.9, s32[1,1024]{1,0:T(1,128)} %refs_3_.1, s32[1,768]{1,0:T(1,128)} %refs_4_.1, s32[1,4,8]{2,1,0:T(4,128)} %bitcast.10, s32[1,8]{1,0:T(1,128)} %refs_6_.1, ...), custom_call_target="tpu_custom_call" | custom-call | tf_op jit(solution)/shard_map/md_step/pallas_call | solution.py:453
  39.3 0.0 copy-start
  39.3 0.8 %copy-done = f32[9,1,1024]{2,1,0:T(1,128)S(1)} copy-done((f32[9,1,1024]{2,1,0:T(1,128)S(1)}, f32[9,1,1024]{2,1,0:T(1,128)}, u32[]{:S(2)}) %copy-start) | copy-done | bytes 36888
  40.1 0.6 %hand_out.1 = (f32[3,1,1024]{2,1,0:T(1,128)}, f32[3,1,1024]{2,1,0:T(1,128)}, f32[3,1,1024]{2,1,0:T(1,128)}) custom-call(f32[9,1,1024]{2,1,0:T(1,128)S(1)} %copy-done), custom_call_target="tpu_custom_call" | custom-call | tf_op jit(solution)/shard_map/hand_out/pallas_call | solution.py:495
Async XLA Ops:
  39.3 0.8 %copy-start = (f32[9,1,1024]{2,1,0:T(1,128)S(1)}, f32[9,1,1024]{2,1,0:T(1,128)}, u32[]{:S(2)}) copy-start(f32[9,1,1024]{2,1,0:T(1,128)} %md_step.1.packed) | copy-start | bytes 110596

commit v5 on v4

--- a/solution.py
+++ b/solution.py
@@ -226,10 +226,11 @@
 
     to_smem.wait()
 
-    def fill_basis(t, buffer, slot):
-        for axis in range(3):
-            xcol[t, axis] = columns(posext[t, 4 + axis : 5 + axis, :])
-        for k in range(NEI):
+    def fill_basis(t, buffer, slot, slots):
+        if 0 in slots:
+            for axis in range(3):
+                xcol[t, axis] = columns(posext[t, 4 + axis : 5 + axis, :])
+        for k in slots:
             far = posext[aux_smem[k, t]]
             dead = jnp.clip(k + 1 - aux_smem[NEI, t], 0, 1).astype(jnp.float32) * FAR
             xj, yj, zj = far[4:5, :] + dead, far[5:6, :], far[6:7, :]
@@ -248,13 +249,19 @@
                     if b:
                         g = g * q
 
-    def sum_messages(layer, t, buffer, slot, source, parity):
-        for k in range(NEI):
-            hcat[parity, k * TILE : (k + 1) * TILE, :] = source[aux_smem[k, t]]
+    def sum_messages(layer, t, buffer, slot, source, parity, bs):
+        if 0 in bs:
+            for k in range(NEI):
+                hcat[parity, k * TILE : (k + 1) * TILE, :] = source[aux_smem[k, t]]
+        low, high = bs[0], bs[-1] + 1
         parts = []
         for k in range(0, NEI, 2):
             flat = jnp.concatenate(
-                [buffer[slot, k + i].reshape(NB * TILE, TILE) for i in range(2)], axis=1
+                [
+                    buffer[slot, k + i, low:high].reshape((high - low) * TILE, TILE)
+                    for i in range(2)
+                ],
+                axis=1,
             )
             parts.append(
                 jnp.dot(
@@ -265,10 +272,12 @@
             )
         summed = parts[0] + parts[1]
         weights = radial[layer]
-        messages = weights[0:1, :] * summed[0:TILE, :]
-        for b in range(1, NB):
-            messages = messages + weights[b : b + 1, :] * summed[b * TILE : (b + 1) * TILE, :]
-        msgs[parity] = messages
+        total = None if low == 0 else msgs[parity]
+        for b in bs:
+            row = b - low
+            term = weights[b : b + 1, :] * summed[row * TILE : (row + 1) * TILE, :]
+            total = term if total is None else total + term
+        msgs[parity] = total
 
     def refresh(layer, t, source, parity):
         messages = msgs[parity]
@@ -282,29 +291,45 @@
 
     halves = (even, odd)
 
-    def fill(t, u, parity):
-        fill_basis(t, halves[parity], u)
+    def fill(t, u, parity, slots=range(NEI)):
+        fill_basis(t, halves[parity], u, slots)
 
     def run_layer(layer, source, finish, prepare):
-        def gather(t, u, parity):
-            sum_messages(layer, t, halves[parity], u, source, parity)
+        def gather(t, u, parity, bs=range(NB)):
+            sum_messages(layer, t, halves[parity], u, source, parity, bs)
 
         def end(t, parity):
             finish(t, refresh(layer, t, source, parity))
 
         if prepare:
-            fill(1, 0, 1)
-        gather(0, 0, 0)
+            fill(1, 0, 1, range(0, 2))
+            gather(0, 0, 0, range(0, 4))
+            fill(1, 0, 1, range(2, 4))
+            gather(0, 0, 0, range(4, 8))
+        else:
+            gather(0, 0, 0)
 
         def pair(u, _):
             if prepare:
-                fill(2 * u + 2, u + 1, 0)
-            gather(2 * u + 1, u, 1)
-            end(2 * u, 0)
+                fill(2 * u + 2, u + 1, 0, range(0, 2))
+                gather(2 * u + 1, u, 1, range(0, 4))
+                fill(2 * u + 2, u + 1, 0, range(2, 4))
+                gather(2 * u + 1, u, 1, range(4, 8))
+                end(2 * u, 0)
+            else:
+                gather(2 * u + 1, u, 1, range(0, 4))
+                end(2 * u, 0)
+                gather(2 * u + 1, u, 1, range(4, 8))
             if prepare:
-                fill(2 * u + 3, u + 1, 1)
-            gather(2 * u + 2, u + 1, 0)
-            end(2 * u + 1, 1)
+                fill(2 * u + 3, u + 1, 1, range(0, 2))
+                gather(2 * u + 2, u + 1, 0, range(0, 4))
+                fill(2 * u + 3, u + 1, 1, range(2, 4))
+                gather(2 * u + 2, u + 1, 0, range(4, 8))
+                end(2 * u + 1, 1)
+            else:
+                gather(2 * u + 2, u + 1, 0, range(0, 4))
+                end(2 * u + 1, 1)
+                gather(2 * u + 2, u + 1, 0, range(4, 8))
             return 0
 
         lax.fori_loop(0, TILES // 2 - 1, pair, 0)

time: 41 us -> 40 us (0.976)
  Pallas kernels: 39.3 us -> 38.3 us
    pallas_call x1, Pallas kernels: 38.7 us -> 37.7 us  [local(): pl.pallas_call(kernel, out_shape=jax.ShapeDtypeStruct((9, 1, ATOMS), jnp....]
where the time goes in v5:
time: 40 us; the launch traced here: 39.7 us
  Pallas kernels  38.3 us (96%)
  local copies, waits for them, and re-layouts  0.76 us (2%)
  between operations  0.65 us (2%)
    pallas_call x1, Pallas kernels, local(): pl.pallas_call(kernel, out_shape=jax.ShapeDtypeStruct((9, 1, ATOMS), jnp....  37.7 us

profile of v5, /device:TPU:1, one launch (start us, length us, event | category | flops | bytes accessed | tf_op | source)
XLA Modules:
  0.0 39.7 jit_solution(8209587601158197312)
XLA Ops:
  0.6 37.7 %md_step.1.packed = f32[9,1,1024]{2,1,0:T(1,128)} custom-call(f32[3,1,1024]{2,1,0:T(1,128)} %bitcast.7, f32[3,1,1024]{2,1,0:T(1,128)} %bitcast.8, f32[3,1,1024]{2,1,0:T(1,128)} %bitcast.9, s32[1,1024]{1,0:T(1,128)} %refs_3_.1, s32[1,768]{1,0:T(1,128)} %refs_4_.1, s32[1,4,8]{2,1,0:T(4,128)} %bitcast.10, s32[1,8]{1,0:T(1,128)} %refs_6_.1, ...), custom_call_target="tpu_custom_call" | custom-call | tf_op jit(solution)/shard_map/md_step/pallas_call | solution.py:478
  38.3 0.0 copy-start
  38.3 0.8 %copy-done = f32[9,1,1024]{2,1,0:T(1,128)S(1)} copy-done((f32[9,1,1024]{2,1,0:T(1,128)S(1)}, f32[9,1,1024]{2,1,0:T(1,128)}, u32[]{:S(2)}) %copy-start) | copy-done | bytes 36888
  39.1 0.6 %hand_out.1 = (f32[3,1,1024]{2,1,0:T(1,128)}, f32[3,1,1024]{2,1,0:T(1,128)}, f32[3,1,1024]{2,1,0:T(1,128)}) custom-call(f32[9,1,1024]{2,1,0:T(1,128)S(1)} %copy-done), custom_call_target="tpu_custom_call" | custom-call | tf_op jit(solution)/shard_map/hand_out/pallas_call | solution.py:520
Async XLA Ops:
  38.3 0.8 %copy-start = (f32[9,1,1024]{2,1,0:T(1,128)S(1)}, f32[9,1,1024]{2,1,0:T(1,128)}, u32[]{:S(2)}) copy-start(f32[9,1,1024]{2,1,0:T(1,128)} %md_step.1.packed) | copy-start | bytes 110596
